TPU v7x, 512 devices: a whole 4x8x8 slice. The times are simulated.
512 devices in a mesh: rx: 64 (over y_lo, z, core), shot: 8 (over y_hi, x).
Axes of the slice: x: 4, y: 8 (y_hi: 2, y_lo: 4; y = y_hi * 4 + y_lo), z: 8, core: 2. Of those that a mesh axis runs over, the one named last changes fastest.
Arguments:
- data: bfloat16 [3, 2, 4, 128, 512, 128], P(None, None, None, 'rx', 'shot'), may hold values from -6 to 6
- mixing: float32 [3, 2, 4, 4, 128, 128], P(None, None, None, None, 'rx'), may hold values from -3 to 3
- counts: int32 [3, 128], P(None, 'rx'), may hold values from 0 to 64
Outputs:
- fields: bfloat16 [3, 2, 4, 128, 512, 128], P(None, None, None, 'rx', 'shot')
- gram: float32 [3, 2, 128, 128, 128], P(None, None, 'rx', 'shot')
All inputs are finite; a program needn't handle non-finite values.
Results may differ from a plain program's by a relative error of at most 0.0091.
Values may be sent and summed in bfloat16 or wider, within the bound.
No kernel may reach another device: no remote copies, remote signals or barrier semaphores. Data moves between devices by JAX's collectives and lax.ppermute only.
A program may use at most 64 MiB of HBM per device.

v0:
```python
import math

import jax
import jax.numpy as jnp
from jax import lax
from jax.sharding import PartitionSpec as P


def in_blocks(array, dim, size):
    before, after = (array.shape[:dim], array.shape[dim + 1 :])
    return jnp.moveaxis(array.reshape(*before, size, -1, *after), dim, 0)


def sum_at_owner(array, axis, dim):
    size = lax.axis_size(axis)
    parts = lax.all_to_all(in_blocks(array, dim, size), axis, 0, 0, tiled=True)
    return jnp.sum(parts, axis=0)


def dft_table(size, sign):
    steps = jnp.arange(size, dtype=jnp.int32)
    phases = steps[:, None] * steps[None, :] % size
    angles = phases.astype(jnp.float32) * (2.0 * math.pi / size)
    factor = 1.0 / math.sqrt(size)
    cosine = jnp.cos(angles) * factor
    sine = jnp.sin(angles) * (factor * sign)
    top_rows = jnp.stack([cosine, -sine], axis=1)
    low_rows = jnp.stack([sine, cosine], axis=1)
    return jnp.stack([top_rows, low_rows], axis=0).astype(jnp.bfloat16)


def apply_mix(matrix, values):
    return jnp.einsum("foikq,fikqs->fokqs", matrix, values, precision=lax.Precision.HIGHEST)


def per_device(data, mixing, counts):
    rx_size = mixing.shape[5]
    ry_size = data.shape[5]
    shots_here = data.shape[4]
    ry_forward = dft_table(ry_size, 1.0)
    rx_forward = dft_table(rx_size, 1.0)
    rx_inverse = dft_table(rx_size, -1.0)
    ry_inverse = dft_table(ry_size, -1.0)
    spectra = jnp.einsum(
        "fcmlsy,cydk->fdmkls", data, ry_forward, preferred_element_type=jnp.float32
    ).astype(jnp.bfloat16)
    pencils = lax.all_to_all(spectra, "rx", split_axis=3, concat_axis=4, tiled=True)
    kspace = jnp.einsum(
        "fcmkxs,cxdq->fdmkqs", pencils, rx_forward, preferred_element_type=jnp.float32
    )
    wave_index = jnp.arange(rx_size, dtype=jnp.int32)
    radial = jnp.minimum(wave_index, rx_size - wave_index)
    passing = (radial[None, None, :] <= counts[:, :, None]).astype(jnp.float32)
    mixed_real = apply_mix(mixing[:, 0], kspace[:, 0]) - apply_mix(mixing[:, 1], kspace[:, 1])
    mixed_imag = apply_mix(mixing[:, 0], kspace[:, 1]) + apply_mix(mixing[:, 1], kspace[:, 0])
    mixed = (
        jnp.stack([mixed_real, mixed_imag], axis=1) * passing[:, None, None, :, :, None]
    ).astype(jnp.bfloat16)
    spaced = jnp.einsum(
        "fcmkqs,cqdx->fdmkxs", mixed, rx_inverse, preferred_element_type=jnp.float32
    ).astype(jnp.bfloat16)
    downgo = spaced[:, :, 1]
    weight = 1.0 / (shots_here * lax.axis_size("shot"))
    product = jnp.einsum("fckxs,fdkzs->xfcdkz", downgo, downgo, preferred_element_type=jnp.float32)
    gram_rows = sum_at_owner(
        jnp.stack(
            [product[:, :, 0, 0] + product[:, :, 1, 1], product[:, :, 1, 0] - product[:, :, 0, 1]],
            axis=2,
        )
        * weight,
        "shot",
        0,
    )
    gram = jnp.transpose(gram_rows, (1, 2, 3, 0, 4))
    returned = lax.all_to_all(spaced, "rx", split_axis=4, concat_axis=3, tiled=True)
    fields = jnp.einsum(
        "fcmkls,ckdy->fdmlsy", returned, ry_inverse, preferred_element_type=jnp.float32
    ).astype(jnp.bfloat16)
    return (fields, gram)


def solution(mesh):
    placed = (
        P(None, None, None, "rx", "shot", None),
        P(None, None, None, None, "rx", None),
        P(None, "rx"),
    )
    return jax.shard_map(
        per_device,
        mesh=mesh,
        in_specs=placed,
        out_specs=(P(None, None, None, "rx", "shot", None), P(None, None, "rx", "shot", None)),
        check_vma=False,
    )
```

profile of v0, /device:TPU:1, one launch (start us, length us, event | category | flops | bytes accessed | tf_op | source)
XLA Modules:
  0.0 161.9 jit_solution(4184178813290754073)
XLA Ops:
  1.5 1.5 fusion.13
  3.0 1.4 copy.72
  4.5 1.7 %reshape.168 = bf16[64,2,3072]{2,1,0:T(2,128)(2,1)} reshape(bf16[128,2,3,4,2,64]{5,4,3,2,1,0:T(2,128)(2,1)S(1)} %bitcast.118) | data formatting | bytes 1572864
  6.1 15.6 %all-to-all-start = ((bf16[64,2,3072]{2,1,0:T(2,128)(2,1)}), bf16[64,2,3072]{2,1,0:T(2,128)(2,1)}, u32[]{:S(2)}, u32[]{:S(2)}) async-start(bf16[64,2,3072]{2,1,0:T(2,128)(2,1)} %reshape.168), calls=%async_computation | async-start | bytes 1572864 | tf_op jit(solution)/shard_map/all_to_all | solution.py:47
  21.8 1.2 copy.127
  23.1 1.2 copy.126
  24.4 20.2 %all-to-all-done = bf16[64,2,3072]{2,1,0:T(2,128)(2,1)} async-done(((bf16[64,2,3072]{2,1,0:T(2,128)(2,1)}), bf16[64,2,3072]{2,1,0:T(2,128)(2,1)}, u32[]{:S(2)}, u32[]{:S(2)}) %all-to-all-start) | async-done | bytes 786464 | tf_op jit(solution)/shard_map/all_to_all | solution.py:47
  44.6 4.7 %reshape.169 = bf16[128,2,3,4,2,64]{5,4,3,2,1,0:T(2,128)(2,1)} reshape(bf16[64,2,3072]{2,1,0:T(2,128)(2,1)} %all-to-all-done) | data formatting | bytes 1572864
  49.3 1.8 %copy.73 = bf16[3,2,4,128,2,64]{5,3,4,2,1,0:T(8,128)(2,1)S(1)} copy(bf16[3,2,4,128,2,64]{5,4,2,0,1,3:T(2,128)(2,1)} %bitcast.119) | data formatting | bytes 1572864 | tf_op jit(solution)/shard_map/all_to_all | solution.py:47
  51.1 2.5 %copy.74 = bf16[3,2,4,2,64,2,64]{6,5,4,3,2,1,0:T(2,128)(2,1)S(1)} copy(bf16[3,2,4,2,64,2,64]{6,3,4,5,2,1,0:T(2,128)(2,1)S(1)} %bitcast.120) | data formatting | bytes 1572864 | tf_op jit(solution)/shard_map/all_to_all | solution.py:47
  54.3 1.3 slice_bitcast_fusion.1
  55.6 2.4 %copy.77 = f32[3,4,2,128,64]{4,1,3,2,0:T(4,128)} copy(f32[3,4,2,128,64]{3,4,2,1,0:T(8,128)} %get-tuple-element.12) | data formatting | bytes 1572864 | tf_op jit(solution)/shard_map/squeeze | solution.py:54
  58.0 2.5 %copy.79 = f32[3,4,2,128,64]{4,1,3,2,0:T(4,128)} copy(f32[3,4,2,128,64]{3,4,2,1,0:T(8,128)} %get-tuple-element.13) | data formatting | bytes 1572864 | tf_op jit(solution)/shard_map/squeeze | solution.py:54
  60.5 7.6 %fusion.7 = f32[3,2,128,64,4]{3,4,2,1,0:T(4,128)} fusion(f32[3,4,2,128,64]{4,1,3,2,0:T(4,128)} %copy.79, f32[3,1,4,4,2,128]{3,2,5,4,0,1:T(4,128)S(1)} %copy.126), kind=kOutput, calls=%fused_computation.10 | convolution fusion | flops 9437184 | bytes 1622016 | tf_op jit(solution)/shard_map/foikq,fikqs->fokqs/dot_general | solution.py:33
  68.1 6.4 %fusion.9 = f32[3,2,128,64,4]{3,4,2,1,0:T(4,128)} fusion(f32[3,4,2,128,64]{4,1,3,2,0:T(4,128)S(1)} %copy-done, f32[3,1,4,4,2,128]{3,2,5,4,0,1:T(4,128)S(1)} %copy.126), kind=kOutput, calls=%fused_computation.12 | convolution fusion | flops 9437184 | bytes 1622016 | tf_op jit(solution)/shard_map/foikq,fikqs->fokqs/dot_general | solution.py:33
  74.5 5.4 %fusion.3 = f32[3,2,128,64,4]{3,4,2,1,0:T(4,128)S(1)} fusion(f32[3,4,2,128,64]{4,1,3,2,0:T(4,128)S(1)} %copy-done, f32[3,1,4,4,2,128]{3,2,5,4,0,1:T(4,128)S(1)} %copy.127), kind=kOutput, calls=%fused_computation.6 | convolution fusion | flops 9437184 | bytes 1622016 | tf_op jit(solution)/shard_map/foikq,fikqs->fokqs/dot_general | solution.py:33
  79.9 6.4 %fusion.5 = f32[3,2,128,64,4]{3,4,2,1,0:T(4,128)} fusion(f32[3,4,2,128,64]{4,1,3,2,0:T(4,128)S(1)} %copy-done.1, f32[3,1,4,4,2,128]{3,2,5,4,0,1:T(4,128)S(1)} %copy.127), kind=kOutput, calls=%fused_computation.8 | convolution fusion | flops 9437184 | bytes 1622016 | tf_op jit(solution)/shard_map/foikq,fikqs->fokqs/dot_general | solution.py:33
  86.3 2.5 %copy.84 = f32[3,2,128,64,4]{2,3,1,4,0:T(8,128)} copy(f32[3,2,128,64,4]{3,4,2,1,0:T(4,128)} %fusion.7) | data formatting | bytes 1572864 | tf_op jit(solution)/shard_map/foikq,fikqs->fokqs/dot_general | solution.py:33
  88.8 1.4 copy.80
  90.2 2.4 %copy.81 = f32[3,2,128,64,4]{2,3,1,4,0:T(8,128)} copy(f32[3,2,128,64,4]{3,4,2,1,0:T(4,128)} %fusion.5) | data formatting | bytes 1572864 | tf_op jit(solution)/shard_map/foikq,fikqs->fokqs/dot_general | solution.py:33
  93.8 1.3 subtract_bitcast_fusion
  96.1 1.0 copy_multiply_fusion
  97.1 6.6 %all-to-all-start.2 = ((f32[8,16,3,2,2,128]{5,1,4,2,3,0:T(8,128)}), f32[8,16,3,2,2,128]{5,1,4,2,3,0:T(8,128)S(1)}, u32[]{:S(2)}, u32[]{:S(2)}) async-start(f32[8,16,3,2,2,128]{5,1,4,2,3,0:T(8,128)} %copy_multiply_fusion), calls=%async_computation.2 | async-start | bytes 1572864 | tf_op jit(solution)/shard_map/all_to_all | solution.py:16
  103.7 1.4 copy.89
  105.1 1.7 %reshape.170 = bf16[64,2,3072]{2,1,0:T(2,128)(2,1)} reshape(bf16[128,2,3,4,2,64]{5,4,3,2,1,0:T(2,128)(2,1)S(1)} %bitcast.121) | data formatting | bytes 1572864
  106.8 11.9 %all-to-all-done.2 = f32[8,16,3,2,2,128]{5,1,4,2,3,0:T(8,128)S(1)} async-done(((f32[8,16,3,2,2,128]{5,1,4,2,3,0:T(8,128)}), f32[8,16,3,2,2,128]{5,1,4,2,3,0:T(8,128)S(1)}, u32[]{:S(2)}, u32[]{:S(2)}) %all-to-all-start.2) | async-done | bytes 786464 | tf_op jit(solution)/shard_map/all_to_all | solution.py:16
  118.7 14.7 %all-to-all-start.1 = ((bf16[64,2,3072]{2,1,0:T(2,128)(2,1)}), bf16[64,2,3072]{2,1,0:T(2,128)(2,1)S(1)}, u32[]{:S(2)}, u32[]{:S(2)}) async-start(bf16[64,2,3072]{2,1,0:T(2,128)(2,1)} %reshape.170), calls=%async_computation.1 | async-start | bytes 1572864 | tf_op jit(solution)/shard_map/all_to_all | solution.py:75
  133.5 0.6 copy.100
  134.1 22.3 %all-to-all-done.1 = bf16[64,2,3072]{2,1,0:T(2,128)(2,1)S(1)} async-done(((bf16[64,2,3072]{2,1,0:T(2,128)(2,1)}), bf16[64,2,3072]{2,1,0:T(2,128)(2,1)S(1)}, u32[]{:S(2)}, u32[]{:S(2)}) %all-to-all-start.1) | async-done | bytes 786464 | tf_op jit(solution)/shard_map/all_to_all | solution.py:75
  156.4 0.9 reshape.171
  157.8 2.5 %copy.91 = bf16[3,2,4,64,2,2,64]{6,4,3,5,2,1,0:T(2,128)(2,1)S(1)} copy(bf16[3,2,4,64,2,2,64]{6,5,3,4,2,1,0:T(2,128)(2,1)S(1)} %bitcast.123) | data formatting | bytes 1572864 | tf_op jit(solution)/shard_map/all_to_all | solution.py:75
  160.9 1.0 copy.99
  (31 shorter events, 4.9 us)
Async XLA Ops:
  4.4 17.3 %copy-start.6 = (s32[3,2]{0,1:T(2,128)S(1)}, s32[3,2]{0,1:T(2,128)}, u32[]{:S(2)}) copy-start(s32[3,2]{0,1:T(2,128)} %param.5) | copy-start | bytes 76
  4.4 17.4 %copy-start.5 = (f32[3,2,4,4,2,128]{5,4,3,2,1,0:T(2,128)S(1)}, f32[3,2,4,4,2,128]{5,4,3,2,1,0:T(2,128)}, u32[]{:S(2)}) copy-start(f32[3,2,4,4,2,128]{5,4,3,2,1,0:T(2,128)} %param.4) | copy-start | bytes 294916
  6.1 38.5 %all-to-all-start = ((bf16[64,2,3072]{2,1,0:T(2,128)(2,1)}), bf16[64,2,3072]{2,1,0:T(2,128)(2,1)}, u32[]{:S(2)}, u32[]{:S(2)}) async-start(bf16[64,2,3072]{2,1,0:T(2,128)(2,1)} %reshape.168), calls=%async_computation | async-start | bytes 1572864 | tf_op jit(solution)/shard_map/all_to_all | solution.py:47
  60.5 7.6 %copy-start = (f32[3,4,2,128,64]{4,1,3,2,0:T(4,128)S(1)}, f32[3,4,2,128,64]{4,1,3,2,0:T(4,128)}, u32[]{:S(2)}) copy-start(f32[3,4,2,128,64]{4,1,3,2,0:T(4,128)} %copy.77) | copy-start | bytes 2359300
  74.5 5.4 %copy-start.1 = (f32[3,4,2,128,64]{4,1,3,2,0:T(4,128)S(1)}, f32[3,4,2,128,64]{4,1,3,2,0:T(4,128)}, u32[]{:S(2)}) copy-start(f32[3,4,2,128,64]{4,1,3,2,0:T(4,128)} %copy.79) | copy-start | bytes 2359300
  86.3 2.5 %copy-start.2 = (f32[3,2,128,64,4]{3,4,2,1,0:T(4,128)S(1)}, f32[3,2,128,64,4]{3,4,2,1,0:T(4,128)}, u32[]{:S(2)}) copy-start(f32[3,2,128,64,4]{3,4,2,1,0:T(4,128)} %fusion.9) | copy-start | bytes 2359300
  92.6 1.1 copy-start.4
  93.8 1.4 copy-start.3
  97.1 21.6 %all-to-all-start.2 = ((f32[8,16,3,2,2,128]{5,1,4,2,3,0:T(8,128)}), f32[8,16,3,2,2,128]{5,1,4,2,3,0:T(8,128)S(1)}, u32[]{:S(2)}, u32[]{:S(2)}) async-start(f32[8,16,3,2,2,128]{5,1,4,2,3,0:T(8,128)} %copy_multiply_fusion), calls=%async_computation.2 | async-start | bytes 1572864 | tf_op jit(solution)/shard_map/all_to_all | solution.py:16
  118.7 37.7 %all-to-all-start.1 = ((bf16[64,2,3072]{2,1,0:T(2,128)(2,1)}), bf16[64,2,3072]{2,1,0:T(2,128)(2,1)S(1)}, u32[]{:S(2)}, u32[]{:S(2)}) async-start(bf16[64,2,3072]{2,1,0:T(2,128)(2,1)} %reshape.170), calls=%async_computation.1 | async-start | bytes 1572864 | tf_op jit(solution)/shard_map/all_to_all | solution.py:75
where the time goes:
time: 162 us
  waiting for transfers between devices  54.4 us (34%)
  local copies, waits for them, and re-layouts  36.9 us (23%)
  starting transfers between devices  36.8 us (23%)
  matrix products  29.4 us (18%)
  other arithmetic  3.47 us (2%)
    dot_general x4, matrix products, apply_mix(): jnp.einsum('foikq,fikqs->fokqs', matrix, values, precision=lax.Precision....  25.8 us
    all_to_all x1, waiting for transfers between devices, per_device(): lax.all_to_all(spaced, 'rx', split_axis=4, concat_axis=3, tiled=True)  22.3 us
    all_to_all x1, waiting for transfers between devices, per_device(): lax.all_to_all(spectra, 'rx', split_axis=3, concat_axis=4, tiled=True)  20.2 us
    all_to_all x1, starting transfers between devices, per_device(): lax.all_to_all(spectra, 'rx', split_axis=3, concat_axis=4, tiled=True)  15.6 us
    all_to_all x1, starting transfers between devices, per_device(): lax.all_to_all(spaced, 'rx', split_axis=4, concat_axis=3, tiled=True)  14.7 us
    unnamed x23, local copies, waits for them, and re-layouts  13.7 us
    all_to_all x1, waiting for transfers between devices, sum_at_owner(): parts = lax.all_to_all(in_blocks(array, dim, size), axis, 0, 0, tiled=True)  11.9 us
    dot_general x4, local copies, waits for them, and re-layouts, apply_mix(): jnp.einsum('foikq,fikqs->fokqs', matrix, values, precision=lax.Precision....  6.93 us
  transfers between devices with their start and end apart: 3, of which 3 were waited for; matrix products, arithmetic and copies ran while one was open for 4% of the time, Pallas kernels for 0%

commit v1 on v0

v1 whole, which is shorter than its diff:
```python
import functools
import math

import jax
import jax.numpy as jnp
import ml_dtypes
import numpy as np
from jax import lax
from jax.experimental import pallas as pl
from jax.experimental.pallas import tpu as pltpu
from jax.sharding import PartitionSpec as P

BF16 = jnp.bfloat16
F32 = jnp.float32
NT = (((1,), (1,)), ((), ()))
NN = (((1,), (0,)), ((), ()))
SX = 4


def dft_table(size, sign):
    steps = np.arange(size, dtype=np.int64)
    angles = (steps[:, None] * steps[None, :] % size).astype(np.float64) * (2.0 * math.pi / size)
    cosine = np.cos(angles) / math.sqrt(size)
    sine = np.sin(angles) * (sign / math.sqrt(size))
    return np.stack(
        [np.stack([cosine, -sine], axis=1), np.stack([sine, cosine], axis=1)], axis=0
    )


def bf16_const(array):
    return np.ascontiguousarray(array).astype(np.float32).astype(ml_dtypes.bfloat16)


def out_rows(table, per):
    n = table.shape[1]
    t = table.reshape(2, n, 2, n // per, per)
    return bf16_const(t.transpose(2, 4, 3, 0, 1).reshape(2 * n, 2 * n))


def in_rows(table, per):
    n = table.shape[1]
    t = table.reshape(2, n // per, per, 2, n)
    return bf16_const(t.transpose(2, 0, 1, 3, 4).reshape(2 * n, 2 * n))


def dot(a, b, dims):
    return lax.dot_general(a, b, dims, preferred_element_type=F32)


def forward_kernel(devices, data_ref, table_ref, out_ref, rows_ref):
    comps = data_ref.shape[2]
    per = rows_ref.shape[0] // devices
    lines = data_ref.shape[3] * data_ref.shape[4]
    size = data_ref.shape[5]
    table = table_ref[...]
    for m in range(comps):
        both = jnp.concatenate(
            [data_ref[0, c, m].reshape(lines, size) for c in range(2)], axis=1
        )
        res = dot(table, both, NT)
        for d in range(2):
            for p in range(2):
                start = (d * 2 + p) * devices
                rows_ref[pl.ds((d * comps + m) * 2 + p, devices, stride=per), :] = res[
                    start : start + devices
                ]
    out_ref[...] = rows_ref[...].reshape(out_ref.shape).astype(BF16)


def gathered(rows_ref, devices, comps, m):
    per = rows_ref.shape[0] // devices
    halves = []
    for p in range(2):
        both = jnp.concatenate(
            [rows_ref[pl.ds((c * comps + m) * 2 + p, devices, stride=per), :] for c in range(2)],
            axis=0,
        )
        turned = both.T.astype(BF16)
        half = turned.shape[0] // 2
        halves.append(jnp.concatenate([turned[:half], turned[half:]], axis=1))
    return jnp.concatenate(halves, axis=0)


def middle_kernel(
    devices, counts_ref, in_ref, mixing_ref, fwd_ref, inv_ref, out_ref, down_ref, rows_ref, k_ref
):
    f = pl.program_id(0)
    comps = mixing_ref.shape[2]
    size = mixing_ref.shape[5]
    per = rows_ref.shape[0] // devices
    rows_ref[...] = in_ref[...].astype(F32).reshape(rows_ref.shape)
    fwd = fwd_ref[...]
    for m in range(comps):
        k_ref[m] = dot(gathered(rows_ref, devices, comps, m), fwd, NN)
    shots = k_ref.shape[1] // 2
    wave = lax.broadcasted_iota(jnp.int32, (1, size), 1)
    radial = jnp.minimum(wave, size - wave)
    inv = inv_ref[...]
    for o in range(comps):
        parts = []
        for p in range(2):
            passing = (radial <= counts_ref[f, p]).astype(F32)
            span = pl.ds(p * shots, shots)
            real = imag = None
            for i in range(comps):
                a = mixing_ref[0, 0, o, i, p : p + 1, :] * passing
                b = mixing_ref[0, 1, o, i, p : p + 1, :] * passing
                kr = k_ref[i, span, 0:size]
                ki = k_ref[i, span, size : 2 * size]
                r = a * kr - b * ki
                s = a * ki + b * kr
                real = r if real is None else real + r
                imag = s if imag is None else imag + s
            parts.append(jnp.concatenate([real, imag], axis=1).astype(BF16))
        mixed = jnp.concatenate(parts, axis=0)
        if o == 1:
            down_ref[0] = mixed
        res = dot(inv, mixed, NT)
        for d in range(2):
            for l in range(2):
                start = (d * 2 + l) * devices
                rows_ref[pl.ds((d * comps + o) * 2 + l, devices, stride=per), :] = res[
                    start : start + devices
                ]
    out_ref[...] = rows_ref[...].reshape(out_ref.shape).astype(BF16)


def gram_kernel(weight, where_ref, down_ref, inv_ref, own_ref, *rest):
    sent, gram_ref = rest[:-1], rest[-1]
    bins = down_ref.shape[0]
    size = down_ref.shape[2] // 2
    slices = own_ref.shape[0] * (1 + len(sent))
    share = size // slices
    inv = inv_ref[...]
    lane = lax.broadcasted_iota(jnp.int32, (1, down_ref.shape[1]), 1)
    shots = down_ref.shape[1] // 2
    for f in range(bins):
        spaced = dot(inv, down_ref[f], NT).astype(BF16)
        real, imag = spaced[:size], spaced[size:]
        zero = jnp.zeros_like(real)
        left = jnp.concatenate([real, imag], axis=1)
        right = jnp.concatenate(
            [left, jnp.concatenate([-imag, real], axis=1)], axis=0
        )
        for p in range(2):
            keep = (lane >= p * shots) & (lane < (p + 1) * shots)
            part = jnp.concatenate(
                [jnp.where(keep, real, zero), jnp.where(keep, imag, zero)], axis=1
            )
            prod = dot(part, right, NT) * weight
            for c in range(2):
                gram_ref[(f * 2 + c) * 2 + p] = prod[:, c * size : (c + 1) * size]
    here_x, here_y = where_ref[0], where_ref[1]
    for t, ref in enumerate((own_ref, *sent)):
        for h in range(own_ref.shape[0]):
            x = lax.rem(here_x + t, SX)
            y = lax.rem(here_y + h, own_ref.shape[0])
            start = pl.multiple_of((y * SX + x) * share, share)
            for g in range(gram_ref.shape[0]):
                ref[h, g * share : (g + 1) * share, :] = gram_ref[
                    g, pl.ds(start, share), :
                ].astype(ref.dtype)


def backward_kernel(devices, in_ref, table_ref, out_ref, rows_ref):
    comps = out_ref.shape[2]
    shots = out_ref.shape[4]
    size = out_ref.shape[5]
    rows_ref[...] = in_ref[...].astype(F32).reshape(rows_ref.shape)
    table = table_ref[...]
    for m in range(comps):
        res = dot(gathered(rows_ref, devices, comps, m), table, NN).astype(BF16)
        for d in range(2):
            for l in range(2):
                out_ref[0, d, m, l] = res[
                    l * shots : (l + 1) * shots, d * size : (d + 1) * size
                ]


def whole(shape):
    return pl.BlockSpec(shape, lambda *_: (0,) * len(shape))


def params():
    return pltpu.CompilerParams(dimension_semantics=("arbitrary",))


def per_device(data, mixing, counts):
    bins, _, comps, lines, shots, ry = data.shape
    rx = mixing.shape[5]
    devices = lax.axis_size("rx")
    shot_devices = lax.axis_size("shot")
    per = 2 * comps * 2
    lanes = lines * shots
    blocks = jax.ShapeDtypeStruct((devices, bins * per, lanes), BF16)
    block = pl.BlockSpec((devices, per, lanes), lambda f: (0, f, 0))
    rows = pltpu.VMEM((devices * per, lanes), F32)
    forward_y = dft_table(ry, 1.0)
    forward_x = dft_table(rx, 1.0)
    inverse_x = dft_table(rx, -1.0)
    inverse_y = dft_table(ry, -1.0)
    table = whole((2 * rx, 2 * rx))
    field = pl.BlockSpec((1,) + data.shape[1:], lambda f: (f, 0, 0, 0, 0, 0))

    sent = pl.pallas_call(
        functools.partial(forward_kernel, devices),
        grid=(bins,),
        out_shape=blocks,
        in_specs=[field, table],
        out_specs=block,
        scratch_shapes=[rows],
        compiler_params=params(),
        name="forward",
    )(data, out_rows(forward_y, 2))
    pencils = lax.all_to_all(sent, "rx", 0, 0, tiled=True)
    spaced, down = pl.pallas_call(
        functools.partial(middle_kernel, devices),
        grid=(bins,),
        out_shape=(blocks, jax.ShapeDtypeStruct((bins, lanes, 2 * rx), BF16)),
        in_specs=[
            pl.BlockSpec(memory_space=pltpu.SMEM),
            block,
            pl.BlockSpec((1,) + mixing.shape[1:], lambda f: (f, 0, 0, 0, 0, 0)),
            table,
            table,
        ],
        out_specs=(block, pl.BlockSpec((1, lanes, 2 * rx), lambda f: (f, 0, 0))),
        scratch_shapes=[rows, pltpu.VMEM((comps, lanes, 2 * rx), F32)],
        compiler_params=params(),
        name="middle",
    )(counts, pencils, mixing, in_rows(forward_x, 2), out_rows(inverse_x, 2))
    returned = lax.all_to_all(spaced, "rx", 0, 0, tiled=True)

    sy = shot_devices // SX
    share = rx // shot_devices
    here = lax.axis_index("shot")
    where = jnp.stack([here % SX, here // SX]).astype(jnp.int32)
    part = (sy, bins * 2 * 2 * share, rx)
    own, *parts = pl.pallas_call(
        functools.partial(gram_kernel, 1.0 / (shots * shot_devices)),
        out_shape=[jax.ShapeDtypeStruct(part, F32)]
        + [jax.ShapeDtypeStruct(part, BF16)] * (SX - 1),
        in_specs=[
            pl.BlockSpec(memory_space=pltpu.SMEM),
            pl.BlockSpec(memory_space=pltpu.VMEM),
            pl.BlockSpec(memory_space=pltpu.VMEM),
        ],
        out_specs=[pl.BlockSpec(memory_space=pltpu.VMEM)] * SX,
        scratch_shapes=[pltpu.VMEM((bins * 2 * 2, rx, rx), F32)],
        cost_estimate=pl.CostEstimate(flops=10**8, bytes_accessed=10**6, transcendentals=0),
        name="gram",
    )(where, down, bf16_const(inverse_x.transpose(2, 3, 0, 1).reshape(2 * rx, 2 * rx)))
    total = own
    for t in range(1, SX):
        pairs = [(s, s // SX * SX + (s % SX + t) % SX) for s in range(shot_devices)]
        total = total + lax.ppermute(parts[t - 1], "shot", pairs).astype(F32)
    gram = total[0]
    for h in range(1, sy):
        pairs = [(s, (s + h * SX) % shot_devices) for s in range(shot_devices)]
        gram = gram + lax.ppermute(total[h].astype(BF16), "shot", pairs).astype(F32)
    gram = gram.reshape(bins, 2, 2, share, rx)

    fields = pl.pallas_call(
        functools.partial(backward_kernel, devices),
        grid=(bins,),
        out_shape=jax.ShapeDtypeStruct(data.shape, BF16),
        in_specs=[block, table],
        out_specs=field,
        scratch_shapes=[rows],
        compiler_params=params(),
        name="backward",
    )(returned, in_rows(inverse_y, 2))
    return (fields, gram)


def solution(mesh):
    placed = (
        P(None, None, None, "rx", "shot", None),
        P(None, None, None, None, "rx", None),
        P(None, "rx"),
    )
    return jax.shard_map(
        per_device,
        mesh=mesh,
        in_specs=placed,
        out_specs=(P(None, None, None, "rx", "shot", None), P(None, None, "rx", "shot", None)),
        check_vma=False,
    )
```

time: 162 us -> 88 us (0.54)
  the two profiles are of different devices: /device:TPU:1 before, /device:TPU:16 now
where the time goes in v1:
time: 88 us; the launch traced here: 87.5 us
  starting transfers between devices  37.5 us (43%)
  waiting for transfers between devices  30 us (34%)
  Pallas kernels  14.4 us (16%)
  local copies, waits for them, and re-layouts  2.44 us (3%)
  other arithmetic  2.28 us (3%)
    all_to_all x1, waiting for transfers between devices, per_device(): pencils = lax.all_to_all(sent, 'rx', 0, 0, tiled=True)  21.5 us
    all_to_all x1, starting transfers between devices, per_device(): pencils = lax.all_to_all(sent, 'rx', 0, 0, tiled=True)  14.5 us
    ppermute x3, starting transfers between devices, per_device(): total = total + lax.ppermute(parts[t - 1], 'shot', pairs).astype(F32)  11.4 us
    all_to_all x1, starting transfers between devices, per_device(): returned = lax.all_to_all(spaced, 'rx', 0, 0, tiled=True)  6.65 us
    ppermute x1, waiting for transfers between devices, per_device(): gram = gram + lax.ppermute(total[h].astype(BF16), 'shot', pairs).astype(F32)  5.17 us
    ppermute x1, starting transfers between devices, per_device(): gram = gram + lax.ppermute(total[h].astype(BF16), 'shot', pairs).astype(F32)  5.04 us
    pallas_call x1, Pallas kernels, per_device(): pl.pallas_call(functools.partial(middle_kernel, devices), grid=(bins,), o...  4.67 us
    pallas_call x1, Pallas kernels, per_device(): pl.pallas_call(functools.partial(forward_kernel, devices), grid=(bins,),...  3.53 us
  transfers between devices with their start and end apart: 6, of which 4 were waited for; matrix products, arithmetic and copies ran while one was open for 3% of the time, Pallas kernels for 3%

profile of v1, /device:TPU:16, one launch (start us, length us, event | category | flops | bytes accessed | tf_op | source)
XLA Modules:
  0.0 87.5 jit_solution(9299269708686805535)
XLA Ops:
  0.6 3.5 %forward.1 = bf16[64,48,128]{2,1,0:T(8,128)(2,1)} custom-call(bf16[3,2,4,2,64,128]{5,4,3,2,1,0:T(8,128)(2,1)} %data_ref.1, bf16[256,256]{1,0:T(8,128)(2,1)} %constant.40.clone.table_ref), custom_call_target="tpu_custom_call" | custom-call | tf_op jit(solution)/shard_map/forward/pallas_call | solution.py:205
  4.2 0.0 copy-start.2
  4.2 14.5 %all-to-all-start = ((bf16[64,48,128]{2,1,0:T(8,128)(2,1)}), bf16[64,48,128]{2,1,0:T(8,128)(2,1)S(1)}, u32[]{:S(2)}, u32[]{:S(2)}) async-start(bf16[64,48,128]{2,1,0:T(8,128)(2,1)} %forward.1), calls=%async_computation | async-start | bytes 1572864 | tf_op jit(solution)/shard_map/all_to_all | solution.py:215
  18.6 0.0 copy-done.2
  18.7 0.7 copy.10.counts_ref
  19.3 21.5 %all-to-all-done.in_ref = bf16[64,48,128]{2,1,0:T(8,128)(2,1)S(1)} async-done(((bf16[64,48,128]{2,1,0:T(8,128)(2,1)}), bf16[64,48,128]{2,1,0:T(8,128)(2,1)S(1)}, u32[]{:S(2)}, u32[]{:S(2)}) %all-to-all-start) | async-done | bytes 786464 | tf_op jit(solution)/shard_map/all_to_all | solution.py:215
  40.8 0.0 copy-start
  40.8 0.9 %copy-done = bf16[64,48,128]{2,1,0:T(8,128)(2,1)} copy-done((bf16[64,48,128]{2,1,0:T(8,128)(2,1)}, bf16[64,48,128]{2,1,0:T(8,128)(2,1)S(1)}, u32[]{:S(2)}) %copy-start) | copy-done | bytes 786456
  41.7 4.7 %middle.1 = (bf16[64,48,128]{2,1,0:T(8,128)(2,1)}, bf16[3,128,256]{2,1,0:T(8,128)(2,1)}) custom-call(s32[3,2]{1,0:T(4,128)} %copy.10.counts_ref, bf16[64,48,128]{2,1,0:T(8,128)(2,1)} %copy-done, f32[3,2,4,4,2,128]{5,4,3,2,1,0:T(2,128)} %mixing_ref.1, bf16[256,256]{1,0:T(8,128)(2,1)} %constant.41.clone.fwd_ref, bf16[256,256]{1,0:T(8,128)(2,1)} %constant.42.clone.inv_ref), custom_call_target="tpu_custom_call" | custom-call | tf_op jit(solution)/shard_map/middle/pallas_call | solution.py:216
  46.4 6.7 %all-to-all-start.1 = ((bf16[64,48,128]{2,1,0:T(8,128)(2,1)}), bf16[64,48,128]{2,1,0:T(8,128)(2,1)S(1)}, u32[]{:S(2)}, u32[]{:S(2)}) async-start(bf16[64,48,128]{2,1,0:T(8,128)(2,1)} %get-tuple-element.8), calls=%async_computation.1 | async-start | bytes 1572864 | tf_op jit(solution)/shard_map/all_to_all | solution.py:232
  53.0 0.7 pad_add_fusion.where_ref
  53.7 2.7 %gram.1 = (f32[2,192,128]{2,1,0:T(8,128)}, bf16[2,192,128]{2,1,0:T(8,128)(2,1)}, bf16[2,192,128]{2,1,0:T(8,128)(2,1)}, bf16[2,192,128]{2,1,0:T(8,128)(2,1)}) custom-call(s32[2]{0:T(128)} %pad_add_fusion.where_ref, bf16[3,128,256]{2,1,0:T(8,128)(2,1)} %get-tuple-element.9.down_ref, bf16[256,256]{1,0:T(8,128)(2,1)} %constant.43.clone.inv_ref), custom_call_target="tpu_custom_call" | custom-call | flops 100000000 | bytes 1000000 | tf_op jit(solution)/shard_map/gram/pallas_call | solution.py:239
  56.4 3.4 %collective-permute-start = (bf16[2,192,128]{2,1,0:T(8,128)(2,1)}, bf16[2,192,128]{2,1,0:T(8,128)(2,1)S(1)}, u32[]{:S(2)}, u32[]{:S(2)}) collective-permute-start(bf16[2,192,128]{2,1,0:T(8,128)(2,1)} %get-tuple-element.11), channel_id=1, source_target_pairs={{0,1},{1,2},{2,3},{3,0},{4,5},{5,6},{6,7},{7,4},{8,9},{9,10},{10,1... | collective-permute-start | bytes 294920 | tf_op jit(solution)/shard_map/ppermute | solution.py:256
  59.8 4.6 %collective-permute-start.1 = (bf16[2,192,128]{2,1,0:T(8,128)(2,1)}, bf16[2,192,128]{2,1,0:T(8,128)(2,1)S(1)}, u32[]{:S(2)}, u32[]{:S(2)}) collective-permute-start(bf16[2,192,128]{2,1,0:T(8,128)(2,1)} %get-tuple-element.12), channel_id=1, source_target_pairs={{0,2},{1,3},{2,0},{3,1},{4,6},{5,7},{6,4},{7,5},{8,10},{9,11},{10,... | collective-permute-start | bytes 294920 | tf_op jit(solution)/shard_map/ppermute | solution.py:256
  64.5 3.3 %collective-permute-start.2 = (bf16[2,192,128]{2,1,0:T(8,128)(2,1)}, bf16[2,192,128]{2,1,0:T(8,128)(2,1)S(1)}, u32[]{:S(2)}, u32[]{:S(2)}) collective-permute-start(bf16[2,192,128]{2,1,0:T(8,128)(2,1)} %get-tuple-element.13), channel_id=1, source_target_pairs={{0,3},{1,0},{2,1},{3,2},{4,7},{5,4},{6,5},{7,6},{8,11},{9,8},{10,9... | collective-permute-start | bytes 294920 | tf_op jit(solution)/shard_map/ppermute | solution.py:256
  67.8 0.0 collective-permute-done
  67.8 0.2 collective-permute-done.1
  68.1 3.1 %collective-permute-done.2 = bf16[2,192,128]{2,1,0:T(8,128)(2,1)S(1)} collective-permute-done((bf16[2,192,128]{2,1,0:T(8,128)(2,1)}, bf16[2,192,128]{2,1,0:T(8,128)(2,1)S(1)}, u32[]{:S(2)}, u32[]{:S(2)}) %collective-permute-start.2) | collective-permute-done | bytes 98336 | tf_op jit(solution)/shard_map/ppermute | solution.py:256
  71.2 1.0 %convert_add_fusion = f32[2,192,128]{2,1,0:T(8,128)S(1)} fusion(bf16[2,192,128]{2,1,0:T(8,128)(2,1)S(1)} %collective-permute-done.2, bf16[2,192,128]{2,1,0:T(8,128)(2,1)S(1)} %collective-permute-done.1, f32[2,192,128]{2,1,0:T(8,128)} %get-tuple-element.10, bf16[2,192,128]{2,1,0:T(8,128)(2,1)S(1)} %collective-permute-done), kind=kLoop, calls=%fused_computation | loop fusion | flops 294912 | bytes 688128 | tf_op jit(solution)/shard_map/add | solution.py:256
  72.2 5.0 %collective-permute-start.3 = (bf16[192,128]{1,0:T(8,128)(2,1)S(1)}, bf16[192,128]{1,0:T(8,128)(2,1)S(1)}, u32[]{:S(2)}, u32[]{:S(2)}) collective-permute-start(bf16[192,128]{1,0:T(8,128)(2,1)S(1)} %fusion.1), channel_id=1, source_target_pairs={{0,4},{1,5},{2,6},{3,7},{4,0},{5,1},{6,2},{7,3},{8,12},{9,13},{10,... | collective-permute-start | bytes 147464 | tf_op jit(solution)/shard_map/ppermute | solution.py:260
  77.2 5.2 %collective-permute-done.3 = bf16[192,128]{1,0:T(8,128)(2,1)S(1)} collective-permute-done((bf16[192,128]{1,0:T(8,128)(2,1)S(1)}, bf16[192,128]{1,0:T(8,128)(2,1)S(1)}, u32[]{:S(2)}, u32[]{:S(2)}) %collective-permute-start.3) | collective-permute-done | bytes 49184 | tf_op jit(solution)/shard_map/ppermute | solution.py:260
  82.4 0.7 fusion
  83.0 0.0 all-to-all-done.1.in_ref
  83.0 0.0 copy-start.1
  83.1 0.9 %copy-done.1 = bf16[64,48,128]{2,1,0:T(8,128)(2,1)} copy-done((bf16[64,48,128]{2,1,0:T(8,128)(2,1)}, bf16[64,48,128]{2,1,0:T(8,128)(2,1)S(1)}, u32[]{:S(2)}) %copy-start.1) | copy-done | bytes 786456
  83.9 3.5 %backward.1 = bf16[3,2,4,2,64,128]{5,4,3,2,1,0:T(8,128)(2,1)} custom-call(bf16[64,48,128]{2,1,0:T(8,128)(2,1)} %copy-done.1, bf16[256,256]{1,0:T(8,128)(2,1)} %constant.44.clone.table_ref), custom_call_target="tpu_custom_call" | custom-call | tf_op jit(solution)/shard_map/backward/pallas_call | solution.py:263
  (1 shorter events, 0.0 us)
Async XLA Ops:
  4.2 14.5 %copy-start.2 = (s32[3,2]{0,1:T(2,128)S(1)}, s32[3,2]{0,1:T(2,128)}, u32[]{:S(2)}) copy-start(s32[3,2]{0,1:T(2,128)} %param.10) | copy-start | bytes 76
  4.2 36.7 %all-to-all-start = ((bf16[64,48,128]{2,1,0:T(8,128)(2,1)}), bf16[64,48,128]{2,1,0:T(8,128)(2,1)S(1)}, u32[]{:S(2)}, u32[]{:S(2)}) async-start(bf16[64,48,128]{2,1,0:T(8,128)(2,1)} %forward.1), calls=%async_computation | async-start | bytes 1572864 | tf_op jit(solution)/shard_map/all_to_all | solution.py:215
  40.8 0.9 %copy-start = (bf16[64,48,128]{2,1,0:T(8,128)(2,1)}, bf16[64,48,128]{2,1,0:T(8,128)(2,1)S(1)}, u32[]{:S(2)}) copy-start(bf16[64,48,128]{2,1,0:T(8,128)(2,1)S(1)} %all-to-all-done.in_ref) | copy-start | bytes 2359300
  46.4 36.7 %all-to-all-start.1 = ((bf16[64,48,128]{2,1,0:T(8,128)(2,1)}), bf16[64,48,128]{2,1,0:T(8,128)(2,1)S(1)}, u32[]{:S(2)}, u32[]{:S(2)}) async-start(bf16[64,48,128]{2,1,0:T(8,128)(2,1)} %get-tuple-element.8), calls=%async_computation.1 | async-start | bytes 1572864 | tf_op jit(solution)/shard_map/all_to_all | solution.py:232
  56.4 11.4 %collective-permute-start = (bf16[2,192,128]{2,1,0:T(8,128)(2,1)}, bf16[2,192,128]{2,1,0:T(8,128)(2,1)S(1)}, u32[]{:S(2)}, u32[]{:S(2)}) collective-permute-start(bf16[2,192,128]{2,1,0:T(8,128)(2,1)} %get-tuple-element.11), channel_id=1, source_target_pairs={{0,1},{1,2},{2,3},{3,0},{4,5},{5,6},{6,7},{7,4},{8,9},{9,10},{10,1... | collective-permute-start | bytes 294920 | tf_op jit(solution)/shard_map/ppermute | solution.py:256
  59.8 8.2 %collective-permute-start.1 = (bf16[2,192,128]{2,1,0:T(8,128)(2,1)}, bf16[2,192,128]{2,1,0:T(8,128)(2,1)S(1)}, u32[]{:S(2)}, u32[]{:S(2)}) collective-permute-start(bf16[2,192,128]{2,1,0:T(8,128)(2,1)} %get-tuple-element.12), channel_id=1, source_target_pairs={{0,2},{1,3},{2,0},{3,1},{4,6},{5,7},{6,4},{7,5},{8,10},{9,11},{10,... | collective-permute-start | bytes 294920 | tf_op jit(solution)/shard_map/ppermute | solution.py:256
  64.5 6.7 %collective-permute-start.2 = (bf16[2,192,128]{2,1,0:T(8,128)(2,1)}, bf16[2,192,128]{2,1,0:T(8,128)(2,1)S(1)}, u32[]{:S(2)}, u32[]{:S(2)}) collective-permute-start(bf16[2,192,128]{2,1,0:T(8,128)(2,1)} %get-tuple-element.13), channel_id=1, source_target_pairs={{0,3},{1,0},{2,1},{3,2},{4,7},{5,4},{6,5},{7,6},{8,11},{9,8},{10,9... | collective-permute-start | bytes 294920 | tf_op jit(solution)/shard_map/ppermute | solution.py:256
  72.2 10.2 %collective-permute-start.3 = (bf16[192,128]{1,0:T(8,128)(2,1)S(1)}, bf16[192,128]{1,0:T(8,128)(2,1)S(1)}, u32[]{:S(2)}, u32[]{:S(2)}) collective-permute-start(bf16[192,128]{1,0:T(8,128)(2,1)S(1)} %fusion.1), channel_id=1, source_target_pairs={{0,4},{1,5},{2,6},{3,7},{4,0},{5,1},{6,2},{7,3},{8,12},{9,13},{10,... | collective-permute-start | bytes 147464 | tf_op jit(solution)/shard_map/ppermute | solution.py:260
  83.0 0.9 %copy-start.1 = (bf16[64,48,128]{2,1,0:T(8,128)(2,1)}, bf16[64,48,128]{2,1,0:T(8,128)(2,1)S(1)}, u32[]{:S(2)}) copy-start(bf16[64,48,128]{2,1,0:T(8,128)(2,1)S(1)} %all-to-all-done.1.in_ref) | copy-start | bytes 2359300

commit v2 on v1

v2 whole, which is shorter than its diff:
```python
import functools
import math

import jax
import jax.numpy as jnp
import ml_dtypes
import numpy as np
from jax import lax
from jax.experimental import pallas as pl
from jax.experimental.pallas import tpu as pltpu
from jax.sharding import PartitionSpec as P


BF16 = jnp.bfloat16
F32 = jnp.float32
NT = (((1,), (1,)), ((), ()))
NN = (((1,), (0,)), ((), ()))
SX = 4
LIMIT = 16 * 2**20


def dft_table(size, sign):
    steps = np.arange(size, dtype=np.int64)
    angles = (steps[:, None] * steps[None, :] % size).astype(np.float64) * (2.0 * math.pi / size)
    cosine = np.cos(angles) / math.sqrt(size)
    sine = np.sin(angles) * (sign / math.sqrt(size))
    return np.stack(
        [np.stack([cosine, -sine], axis=1), np.stack([sine, cosine], axis=1)], axis=0
    )


def bf16_const(array):
    return np.ascontiguousarray(array).astype(np.float32).astype(ml_dtypes.bfloat16)


def out_rows(table, per):
    n = table.shape[1]
    t = table.reshape(2, n, 2, n // per, per)
    return bf16_const(t.transpose(2, 4, 3, 0, 1).reshape(2 * n, 2 * n))


def in_rows(table, per):
    n = table.shape[1]
    t = table.reshape(2, n // per, per, 2, n)
    return bf16_const(t.transpose(2, 0, 1, 3, 4).reshape(2 * n, 2 * n))


def dot(a, b, dims):
    return lax.dot_general(a, b, dims, preferred_element_type=F32)


def spread(rows_ref, devices, comps, f, m, res):
    step = rows_ref.shape[1] // devices
    for d in range(2):
        for p in range(2):
            start = (d * 2 + p) * devices
            rows_ref[f, pl.ds((d * comps + m) * 2 + p, devices, stride=step), :] = res[
                start : start + devices
            ]


def put(out_ref, block_ref, rows_ref, sems, f):
    devices, per = block_ref.shape[1:3]
    step = rows_ref.shape[1] // devices
    for j in range(devices):
        block_ref[f, j] = rows_ref[f, j * step : j * step + per, :].astype(BF16)
    copy = pltpu.make_async_copy(
        block_ref.at[f], out_ref.at[:, f * per : (f + 1) * per, :], sems.at[f]
    )
    copy.start()
    return copy


def take(rows_ref, in_ref, per, f):
    devices = in_ref.shape[0]
    step = rows_ref.shape[1] // devices
    for j in range(devices):
        rows_ref[f, j * step : j * step + per, :] = in_ref[j, f * per : (f + 1) * per, :].astype(F32)


def gathered(rows_ref, devices, comps, f, m):
    step = rows_ref.shape[1] // devices
    halves = []
    for p in range(2):
        both = jnp.concatenate(
            [rows_ref[f, pl.ds((c * comps + m) * 2 + p, devices, stride=step), :] for c in range(2)],
            axis=0,
        )
        turned = both.T.astype(BF16)
        half = turned.shape[0] // 2
        halves.append(jnp.concatenate([turned[:half], turned[half:]], axis=1))
    return jnp.concatenate(halves, axis=0)


def forward_kernel(
    devices, data_ref, table_ref, out_ref, in_ref, tab_ref, rows_ref, block_ref, sems, out_sems
):
    bins, _, comps = data_ref.shape[:3]
    lines = data_ref.shape[3] * data_ref.shape[4]
    size = data_ref.shape[5]
    loads = [
        pltpu.make_async_copy(data_ref.at[f], in_ref.at[f], sems.at[f]) for f in range(bins)
    ]
    load_table = pltpu.make_async_copy(table_ref, tab_ref, sems.at[bins])
    loads[0].start()
    load_table.start()
    for load in loads[1:]:
        load.start()
    load_table.wait()
    stores = []
    for f in range(bins):
        loads[f].wait()
        for m in range(comps):
            both = jnp.concatenate(
                [in_ref[f, c, m].reshape(lines, size) for c in range(2)], axis=1
            )
            spread(rows_ref, devices, comps, f, m, dot(tab_ref[...], both, NT))
        stores.append(put(out_ref, block_ref, rows_ref, out_sems, f))
    for store in stores:
        store.wait()


def middle_kernel(
    devices,
    counts_ref,
    in_ref,
    mixing_ref,
    fwd_ref,
    inv_ref,
    out_ref,
    down_ref,
    rows_ref,
    k_ref,
    block_ref,
    out_sems,
):
    bins, _, comps = mixing_ref.shape[:3]
    size = mixing_ref.shape[5]
    shots = in_ref.shape[2] // 2
    wave = lax.broadcasted_iota(jnp.int32, (1, size), 1)
    radial = jnp.minimum(wave, size - wave)
    stores = []
    for f in range(bins):
        take(rows_ref, in_ref, 2 * comps * 2, f)
        for m in range(comps):
            k_ref[f, m] = dot(gathered(rows_ref, devices, comps, f, m), fwd_ref[...], NN)
        for o in range(comps):
            parts = []
            for p in range(2):
                passing = (radial <= counts_ref[f, p]).astype(F32)
                span = pl.ds(p * shots, shots)
                real = imag = None
                for i in range(comps):
                    a = mixing_ref[f, 0, o, i, p : p + 1, :] * passing
                    b = mixing_ref[f, 1, o, i, p : p + 1, :] * passing
                    kr = k_ref[f, i, span, 0:size]
                    ki = k_ref[f, i, span, size : 2 * size]
                    r = a * kr - b * ki
                    s = a * ki + b * kr
                    real = r if real is None else real + r
                    imag = s if imag is None else imag + s
                parts.append(jnp.concatenate([real, imag], axis=1).astype(BF16))
            mixed = jnp.concatenate(parts, axis=0)
            if o == 1:
                down_ref[f] = mixed
            spread(rows_ref, devices, comps, f, o, dot(inv_ref[...], mixed, NT))
        stores.append(put(out_ref, block_ref, rows_ref, out_sems, f))
    for store in stores:
        store.wait()


def gram_kernel(weight, down_ref, inv_ref, own_ref, *rest):
    sent, gram_ref = rest[:-1], rest[-1]
    bins = down_ref.shape[0]
    size = down_ref.shape[2] // 2
    sy = own_ref.shape[0]
    share = size // (sy * SX)
    here = lax.axis_index("shot")
    here_x, here_y = lax.rem(here, SX), lax.div(here, SX)
    lane = lax.broadcasted_iota(jnp.int32, (1, down_ref.shape[1]), 1)
    shots = down_ref.shape[1] // 2
    for f in range(bins):
        spaced = dot(inv_ref[...], down_ref[f], NT).astype(BF16)
        real, imag = spaced[:size], spaced[size:]
        zero = jnp.zeros_like(real)
        left = jnp.concatenate([real, imag], axis=1)
        right = jnp.concatenate([left, jnp.concatenate([-imag, real], axis=1)], axis=0)
        for p in range(2):
            keep = (lane >= p * shots) & (lane < (p + 1) * shots)
            part = jnp.concatenate(
                [jnp.where(keep, real, zero), jnp.where(keep, imag, zero)], axis=1
            )
            prod = dot(part, right, NT) * weight
            for c in range(2):
                gram_ref[(f * 2 + c) * 2 + p] = prod[:, c * size : (c + 1) * size]
    for t, ref in enumerate((own_ref, *sent)):
        for h in range(sy):
            x = lax.rem(here_x + t, SX)
            y = lax.rem(here_y + h, sy)
            start = pl.multiple_of((y * SX + x) * share, share)
            for g in range(gram_ref.shape[0]):
                ref[h, g * share : (g + 1) * share, :] = gram_ref[
                    g, pl.ds(start, share), :
                ].astype(ref.dtype)


def backward_kernel(devices, in_ref, table_ref, out_ref, rows_ref, res_ref, sems):
    bins, _, comps, lines, shots, size = out_ref.shape
    stores = []
    for f in range(bins):
        take(rows_ref, in_ref, 2 * comps * 2, f)
        for m in range(comps):
            res = dot(gathered(rows_ref, devices, comps, f, m), table_ref[...], NN).astype(BF16)
            for d in range(2):
                for l in range(lines):
                    res_ref[f, d, m, l] = res[
                        l * shots : (l + 1) * shots, d * size : (d + 1) * size
                    ]
            store = pltpu.make_async_copy(
                res_ref.at[f, :, m], out_ref.at[f, :, m], sems.at[f * comps + m]
            )
            store.start()
            stores.append(store)
    for store in stores:
        store.wait()


def params():
    return pltpu.CompilerParams(vmem_limit_bytes=LIMIT)


def per_device(data, mixing, counts):
    bins, _, comps, lines, shots, ry = data.shape
    rx = mixing.shape[5]
    devices = lax.axis_size("rx")
    shot_devices = lax.axis_size("shot")
    per = 2 * comps * 2
    lanes = lines * shots
    blocks = jax.ShapeDtypeStruct((devices, bins * per, lanes), BF16)
    rows = pltpu.VMEM((bins, devices * (per + 1), lanes), F32)
    block = pltpu.VMEM((bins, devices, per, lanes), BF16)
    forward_y = dft_table(ry, 1.0)
    forward_x = dft_table(rx, 1.0)
    inverse_x = dft_table(rx, -1.0)
    inverse_y = dft_table(ry, -1.0)
    vmem = pl.BlockSpec(memory_space=pltpu.VMEM)
    outside = pl.BlockSpec(memory_space=pl.ANY)
    fields_shape = jax.ShapeDtypeStruct(data.shape, BF16)

    sent = pl.pallas_call(
        functools.partial(forward_kernel, devices),
        out_shape=blocks,
        in_specs=[outside, outside],
        out_specs=outside,
        scratch_shapes=[
            pltpu.VMEM(data.shape, BF16),
            pltpu.VMEM((2 * ry, 2 * ry), BF16),
            rows,
            block,
            pltpu.SemaphoreType.DMA((bins + 1,)),
            pltpu.SemaphoreType.DMA((bins,)),
        ],
        name="forward",
    )(data, out_rows(forward_y, 2))
    pencils = lax.all_to_all(sent, "rx", 0, 0, tiled=True)
    spaced, down = pl.pallas_call(
        functools.partial(middle_kernel, devices),
        out_shape=(blocks, jax.ShapeDtypeStruct((bins, lanes, 2 * rx), BF16)),
        in_specs=[pl.BlockSpec(memory_space=pltpu.SMEM), vmem, vmem, vmem, vmem],
        out_specs=(outside, vmem),
        scratch_shapes=[
            rows,
            pltpu.VMEM((bins, comps, lanes, 2 * rx), F32),
            block,
            pltpu.SemaphoreType.DMA((bins,)),
        ],
        compiler_params=params(),
        name="middle",
    )(counts, pencils, mixing, in_rows(forward_x, 2), out_rows(inverse_x, 2))
    returned = lax.all_to_all(spaced, "rx", 0, 0, tiled=True)

    sy = shot_devices // SX
    share = rx // shot_devices
    part = (sy, bins * 2 * 2 * share, rx)
    own, *parts = pl.pallas_call(
        functools.partial(gram_kernel, 1.0 / (shots * shot_devices)),
        out_shape=[jax.ShapeDtypeStruct(part, F32)]
        + [jax.ShapeDtypeStruct(part, BF16)] * (SX - 1),
        in_specs=[vmem, vmem],
        out_specs=[vmem] * SX,
        scratch_shapes=[pltpu.VMEM((bins * 2 * 2, rx, rx), F32)],
        compiler_params=params(),
        cost_estimate=pl.CostEstimate(flops=10**8, bytes_accessed=10**6, transcendentals=0),
        name="gram",
    )(down, bf16_const(inverse_x.transpose(2, 3, 0, 1).reshape(2 * rx, 2 * rx)))
    total = own
    for t in range(1, SX):
        pairs = [(s, s // SX * SX + (s % SX + t) % SX) for s in range(shot_devices)]
        total = total + lax.ppermute(parts[t - 1], "shot", pairs).astype(F32)
    gram = total[0]
    for h in range(1, sy):
        pairs = [(s, (s + h * SX) % shot_devices) for s in range(shot_devices)]
        far = lax.ppermute(total[h].astype(BF16), "shot", pairs)
        gram = gram + far.astype(F32)
    gram = gram.reshape(bins, 2, 2, share, rx)

    fields_of = pl.pallas_call(
        functools.partial(backward_kernel, devices),
        out_shape=fields_shape,
        in_specs=[vmem, vmem],
        out_specs=outside,
        scratch_shapes=[rows, pltpu.VMEM(data.shape, BF16), pltpu.SemaphoreType.DMA((bins * comps,))],
        compiler_params=params(),
        name="backward",
    )
    fields = fields_of(returned, in_rows(inverse_y, 2))
    return (fields, gram)


def solution(mesh):
    placed = (
        P(None, None, None, "rx", "shot", None),
        P(None, None, None, None, "rx", None),
        P(None, "rx"),
    )

    return jax.shard_map(
        per_device,
        mesh=mesh,
        in_specs=placed,
        out_specs=(P(None, None, None, "rx", "shot", None), P(None, None, "rx", "shot", None)),
        check_vma=False,
    )
```

time: 88 us -> 78.5 us (0.89)
  the two profiles are of different devices: /device:TPU:16 before, /device:TPU:8 now
where the time goes in v2:
time: 78.5 us; the launch traced here: 78.1 us
  starting transfers between devices  38.5 us (49%)
  waiting for transfers between devices  29.7 us (38%)
  Pallas kernels  8.22 us (10%)
  between operations  0.79 us (1%)
    all_to_all x1, waiting for transfers between devices, per_device(): pencils = lax.all_to_all(sent, 'rx', 0, 0, tiled=True)  21.4 us
    all_to_all x1, starting transfers between devices, per_device(): pencils = lax.all_to_all(sent, 'rx', 0, 0, tiled=True)  14.5 us
    ppermute x3, starting transfers between devices, per_device(): total = total + lax.ppermute(parts[t - 1], 'shot', pairs).astype(F32)  11.4 us
    all_to_all x1, starting transfers between devices, per_device(): returned = lax.all_to_all(spaced, 'rx', 0, 0, tiled=True)  7.43 us
    ppermute x1, starting transfers between devices, per_device(): far = lax.ppermute(total[h].astype(BF16), 'shot', pairs)  5.17 us
    ppermute x1, waiting for transfers between devices, per_device(): far = lax.ppermute(total[h].astype(BF16), 'shot', pairs)  5.13 us
    pallas_call x1, Pallas kernels, per_device(): pl.pallas_call(functools.partial(middle_kernel, devices), out_shape=(bloc...  3.25 us
    ppermute x3, waiting for transfers between devices, per_device(): total = total + lax.ppermute(parts[t - 1], 'shot', pairs).astype(F32)  3.15 us
  transfers between devices with their start and end apart: 6, of which 3 were waited for; matrix products, arithmetic and copies ran while one was open for 1% of the time, Pallas kernels for 1%

profile of v2, /device:TPU:8, one launch (start us, length us, event | category | flops | bytes accessed | tf_op | source)
XLA Modules:
  0.0 78.1 jit_solution(186486995567385719)
XLA Ops:
  0.6 2.7 %forward.1 = bf16[64,48,128]{2,1,0:T(8,128)(2,1)} custom-call(bf16[3,2,4,2,64,128]{5,4,3,2,1,0:T(8,128)(2,1)} %data_ref.1, bf16[256,256]{1,0:T(8,128)(2,1)} %constant.10.clone.table_ref), custom_call_target="tpu_custom_call" | custom-call | tf_op jit(solution)/shard_map/forward/pallas_call | solution.py:250
  3.3 0.0 copy-start.5
  3.3 0.0 copy-start
  3.4 0.0 copy-start.1
  3.4 0.0 copy-start.3
  3.4 14.5 %all-to-all-start = ((bf16[64,48,128]{2,1,0:T(8,128)(2,1)}), bf16[64,48,128]{2,1,0:T(8,128)(2,1)S(1)}, u32[]{:S(2)}, u32[]{:S(2)}) async-start(bf16[64,48,128]{2,1,0:T(8,128)(2,1)} %forward.1), calls=%async_computation | async-start | bytes 1572864 | tf_op jit(solution)/shard_map/all_to_all | solution.py:265
  17.9 0.0 copy-done.5
  17.9 0.1 copy.10.counts_ref
  18.0 21.4 %all-to-all-done.in_ref = bf16[64,48,128]{2,1,0:T(8,128)(2,1)S(1)} async-done(((bf16[64,48,128]{2,1,0:T(8,128)(2,1)}), bf16[64,48,128]{2,1,0:T(8,128)(2,1)S(1)}, u32[]{:S(2)}, u32[]{:S(2)}) %all-to-all-start) | async-done | bytes 786464 | tf_op jit(solution)/shard_map/all_to_all | solution.py:265
  39.4 0.0 copy-done
  39.4 0.0 copy-done.1
  39.4 0.0 copy-done.3
  39.4 3.2 %middle.1 = (bf16[64,48,128]{2,1,0:T(8,128)(2,1)}, bf16[3,128,256]{2,1,0:T(8,128)(2,1)S(1)}) custom-call(s32[3,2]{1,0:T(4,128)S(1)} %copy.10.counts_ref, bf16[64,48,128]{2,1,0:T(8,128)(2,1)S(1)} %all-to-all-done.in_ref, f32[3,2,4,4,2,128]{5,4,3,2,1,0:T(2,128)S(1)} %copy-done.3, bf16[256,256]{1,0:T(8,128)(2,1)S(1)} %copy-done, bf16[256,256]{1,0:T(8,128)(2,1)S(1)} %copy-done.1), custom_call_target="tpu_custom_call" | custom-call | tf_op jit(solution)/shard_map/middle/pallas_call | solution.py:266
  42.7 0.0 copy-start.4
  42.7 7.4 %all-to-all-start.1 = ((bf16[64,48,128]{2,1,0:T(8,128)(2,1)}), bf16[64,48,128]{2,1,0:T(8,128)(2,1)S(1)}, u32[]{:S(2)}, u32[]{:S(2)}) async-start(bf16[64,48,128]{2,1,0:T(8,128)(2,1)} %get-tuple-element.8), calls=%async_computation.1 | async-start | bytes 1572864 | tf_op jit(solution)/shard_map/all_to_all | solution.py:280
  50.2 0.0 copy-done.4
  50.2 1.0 %gram.1 = (f32[2,192,128]{2,1,0:T(8,128)S(1)}, bf16[2,192,128]{2,1,0:T(8,128)(2,1)S(1)}, bf16[2,192,128]{2,1,0:T(8,128)(2,1)S(1)}, bf16[2,192,128]{2,1,0:T(8,128)(2,1)S(1)}) custom-call(bf16[3,128,256]{2,1,0:T(8,128)(2,1)S(1)} %get-tuple-element.9.down_ref, bf16[256,256]{1,0:T(8,128)(2,1)S(1)} %copy-done.4), custom_call_target="tpu_custom_call" | custom-call | flops 100000000 | bytes 1000000 | tf_op jit(solution)/shard_map/gram/pallas_call | solution.py:285
  51.2 3.4 %collective-permute-start = (bf16[2,192,128]{2,1,0:T(8,128)(2,1)S(1)}, bf16[2,192,128]{2,1,0:T(8,128)(2,1)S(1)}, u32[]{:S(2)}, u32[]{:S(2)}) collective-permute-start(bf16[2,192,128]{2,1,0:T(8,128)(2,1)S(1)} %get-tuple-element.11), channel_id=1, source_target_pairs={{0,1},{1,2},{2,3},{3,0},{4,5},{5,6},{6,7},{7,4},{8,9},{9,10},{10,1... | collective-permute-start | bytes 294920 | tf_op jit(solution)/shard_map/ppermute | solution.py:299
  54.6 4.6 %collective-permute-start.1 = (bf16[2,192,128]{2,1,0:T(8,128)(2,1)S(1)}, bf16[2,192,128]{2,1,0:T(8,128)(2,1)S(1)}, u32[]{:S(2)}, u32[]{:S(2)}) collective-permute-start(bf16[2,192,128]{2,1,0:T(8,128)(2,1)S(1)} %get-tuple-element.12), channel_id=1, source_target_pairs={{0,2},{1,3},{2,0},{3,1},{4,6},{5,7},{6,4},{7,5},{8,10},{9,11},{10,... | collective-permute-start | bytes 294920 | tf_op jit(solution)/shard_map/ppermute | solution.py:299
  59.2 3.3 %collective-permute-start.2 = (bf16[2,192,128]{2,1,0:T(8,128)(2,1)S(1)}, bf16[2,192,128]{2,1,0:T(8,128)(2,1)S(1)}, u32[]{:S(2)}, u32[]{:S(2)}) collective-permute-start(bf16[2,192,128]{2,1,0:T(8,128)(2,1)S(1)} %get-tuple-element.13), channel_id=1, source_target_pairs={{0,3},{1,0},{2,1},{3,2},{4,7},{5,4},{6,5},{7,6},{8,11},{9,8},{10,9... | collective-permute-start | bytes 294920 | tf_op jit(solution)/shard_map/ppermute | solution.py:299
  62.6 0.0 collective-permute-done
  62.6 0.0 collective-permute-done.1
  62.6 3.1 %collective-permute-done.2 = bf16[2,192,128]{2,1,0:T(8,128)(2,1)S(1)} collective-permute-done((bf16[2,192,128]{2,1,0:T(8,128)(2,1)S(1)}, bf16[2,192,128]{2,1,0:T(8,128)(2,1)S(1)}, u32[]{:S(2)}, u32[]{:S(2)}) %collective-permute-start.2) | collective-permute-done | bytes 98336 | tf_op jit(solution)/shard_map/ppermute | solution.py:299
  65.8 0.0 copy-start.2
  65.8 5.2 %collective-permute-start.3 = (bf16[192,128]{1,0:T(8,128)(2,1)S(1)}, bf16[192,128]{1,0:T(8,128)(2,1)S(1)}, u32[]{:S(2)}, u32[]{:S(2)}) collective-permute-start(bf16[192,128]{1,0:T(8,128)(2,1)S(1)} %fusion.1), channel_id=1, source_target_pairs={{0,4},{1,5},{2,6},{3,7},{4,0},{5,1},{6,2},{7,3},{8,12},{9,13},{10,... | collective-permute-start | bytes 147464 | tf_op jit(solution)/shard_map/ppermute | solution.py:303
  71.0 5.1 %collective-permute-done.3 = bf16[192,128]{1,0:T(8,128)(2,1)S(1)} collective-permute-done((bf16[192,128]{1,0:T(8,128)(2,1)S(1)}, bf16[192,128]{1,0:T(8,128)(2,1)S(1)}, u32[]{:S(2)}, u32[]{:S(2)}) %collective-permute-start.3) | collective-permute-done | bytes 49184 | tf_op jit(solution)/shard_map/ppermute | solution.py:303
  76.1 0.7 fusion
  76.8 0.0 all-to-all-done.1.in_ref
  76.8 0.0 copy-done.2
  76.8 1.3 %backward.1 = bf16[3,2,4,2,64,128]{5,4,3,2,1,0:T(8,128)(2,1)} custom-call(bf16[64,48,128]{2,1,0:T(8,128)(2,1)S(1)} %all-to-all-done.1.in_ref, bf16[256,256]{1,0:T(8,128)(2,1)S(1)} %copy-done.2), custom_call_target="tpu_custom_call" | custom-call | tf_op jit(solution)/shard_map/backward/pallas_call | solution.py:316
  (2 shorter events, 0.1 us)
Async XLA Ops:
  3.3 14.6 %copy-start.5 = (s32[3,2]{0,1:T(2,128)S(1)}, s32[3,2]{0,1:T(2,128)}, u32[]{:S(2)}) copy-start(s32[3,2]{0,1:T(2,128)} %param.10) | copy-start | bytes 76
  3.3 36.1 %copy-start = (bf16[256,256]{1,0:T(8,128)(2,1)S(1)}, bf16[256,256]{1,0:T(8,128)(2,1)}, u32[]{:S(2)}) copy-start(bf16[256,256]{1,0:T(8,128)(2,1)} %constant.11.clone.fwd_ref) | copy-start | bytes 393220
  3.4 36.1 %copy-start.1 = (bf16[256,256]{1,0:T(8,128)(2,1)S(1)}, bf16[256,256]{1,0:T(8,128)(2,1)}, u32[]{:S(2)}) copy-start(bf16[256,256]{1,0:T(8,128)(2,1)} %constant.12.clone.inv_ref) | copy-start | bytes 393220
  3.4 36.1 %copy-start.3 = (f32[3,2,4,4,2,128]{5,4,3,2,1,0:T(2,128)S(1)}, f32[3,2,4,4,2,128]{5,4,3,2,1,0:T(2,128)}, u32[]{:S(2)}) copy-start(f32[3,2,4,4,2,128]{5,4,3,2,1,0:T(2,128)} %mixing_ref.1) | copy-start | bytes 294916
  3.4 36.1 %all-to-all-start = ((bf16[64,48,128]{2,1,0:T(8,128)(2,1)}), bf16[64,48,128]{2,1,0:T(8,128)(2,1)S(1)}, u32[]{:S(2)}, u32[]{:S(2)}) async-start(bf16[64,48,128]{2,1,0:T(8,128)(2,1)} %forward.1), calls=%async_computation | async-start | bytes 1572864 | tf_op jit(solution)/shard_map/all_to_all | solution.py:265
  42.7 7.5 %copy-start.4 = (bf16[256,256]{1,0:T(8,128)(2,1)S(1)}, bf16[256,256]{1,0:T(8,128)(2,1)}, u32[]{:S(2)}) copy-start(bf16[256,256]{1,0:T(8,128)(2,1)} %constant.13.clone.inv_ref) | copy-start | bytes 393220
  42.7 34.1 %all-to-all-start.1 = ((bf16[64,48,128]{2,1,0:T(8,128)(2,1)}), bf16[64,48,128]{2,1,0:T(8,128)(2,1)S(1)}, u32[]{:S(2)}, u32[]{:S(2)}) async-start(bf16[64,48,128]{2,1,0:T(8,128)(2,1)} %get-tuple-element.8), calls=%async_computation.1 | async-start | bytes 1572864 | tf_op jit(solution)/shard_map/all_to_all | solution.py:280
  51.2 11.4 %collective-permute-start = (bf16[2,192,128]{2,1,0:T(8,128)(2,1)S(1)}, bf16[2,192,128]{2,1,0:T(8,128)(2,1)S(1)}, u32[]{:S(2)}, u32[]{:S(2)}) collective-permute-start(bf16[2,192,128]{2,1,0:T(8,128)(2,1)S(1)} %get-tuple-element.11), channel_id=1, source_target_pairs={{0,1},{1,2},{2,3},{3,0},{4,5},{5,6},{6,7},{7,4},{8,9},{9,10},{10,1... | collective-permute-start | bytes 294920 | tf_op jit(solution)/shard_map/ppermute | solution.py:299
  54.6 8.0 %collective-permute-start.1 = (bf16[2,192,128]{2,1,0:T(8,128)(2,1)S(1)}, bf16[2,192,128]{2,1,0:T(8,128)(2,1)S(1)}, u32[]{:S(2)}, u32[]{:S(2)}) collective-permute-start(bf16[2,192,128]{2,1,0:T(8,128)(2,1)S(1)} %get-tuple-element.12), channel_id=1, source_target_pairs={{0,2},{1,3},{2,0},{3,1},{4,6},{5,7},{6,4},{7,5},{8,10},{9,11},{10,... | collective-permute-start | bytes 294920 | tf_op jit(solution)/shard_map/ppermute | solution.py:299
  59.2 6.5 %collective-permute-start.2 = (bf16[2,192,128]{2,1,0:T(8,128)(2,1)S(1)}, bf16[2,192,128]{2,1,0:T(8,128)(2,1)S(1)}, u32[]{:S(2)}, u32[]{:S(2)}) collective-permute-start(bf16[2,192,128]{2,1,0:T(8,128)(2,1)S(1)} %get-tuple-element.13), channel_id=1, source_target_pairs={{0,3},{1,0},{2,1},{3,2},{4,7},{5,4},{6,5},{7,6},{8,11},{9,8},{10,9... | collective-permute-start | bytes 294920 | tf_op jit(solution)/shard_map/ppermute | solution.py:299
  65.8 11.0 %copy-start.2 = (bf16[256,256]{1,0:T(8,128)(2,1)S(1)}, bf16[256,256]{1,0:T(8,128)(2,1)}, u32[]{:S(2)}) copy-start(bf16[256,256]{1,0:T(8,128)(2,1)} %constant.14.clone.table_ref) | copy-start | bytes 393220
  65.8 10.3 %collective-permute-start.3 = (bf16[192,128]{1,0:T(8,128)(2,1)S(1)}, bf16[192,128]{1,0:T(8,128)(2,1)S(1)}, u32[]{:S(2)}, u32[]{:S(2)}) collective-permute-start(bf16[192,128]{1,0:T(8,128)(2,1)S(1)} %fusion.1), channel_id=1, source_target_pairs={{0,4},{1,5},{2,6},{3,7},{4,0},{5,1},{6,2},{7,3},{8,12},{9,13},{10,... | collective-permute-start | bytes 147464 | tf_op jit(solution)/shard_map/ppermute | solution.py:303

commit v3 on v2

--- a/solution.py
+++ b/solution.py
@@ -16,7 +16,14 @@
 NT = (((1,), (1,)), ((), ()))
 NN = (((1,), (0,)), ((), ()))
 SX = 4
+CHUNK = 8
 LIMIT = 16 * 2**20
+ORDER = [
+    37, 0, 27, 13, 19, 54, 55, 40, 17, 53, 43, 14, 28, 23, 51, 9,
+    52, 62, 44, 50, 25, 10, 63, 6, 20, 16, 61, 32, 56, 45, 7, 36,
+    3, 30, 60, 33, 24, 11, 47, 4, 34, 59, 46, 22, 1, 26, 35, 8,
+    21, 38, 15, 29, 18, 49, 58, 41, 5, 39, 12, 31, 57, 48, 42, 2,
+]
 
 
 def dft_table(size, sign):
@@ -35,13 +42,13 @@
 
 def out_rows(table, per):
     n = table.shape[1]
-    t = table.reshape(2, n, 2, n // per, per)
+    t = table.reshape(2, n, 2, n // per, per)[:, :, :, ORDER]
     return bf16_const(t.transpose(2, 4, 3, 0, 1).reshape(2 * n, 2 * n))
 
 
 def in_rows(table, per):
     n = table.shape[1]
-    t = table.reshape(2, n // per, per, 2, n)
+    t = table.reshape(2, n // per, per, 2, n)[:, ORDER]
     return bf16_const(t.transpose(2, 0, 1, 3, 4).reshape(2 * n, 2 * n))
 
 
@@ -86,7 +93,7 @@
             [rows_ref[f, pl.ds((c * comps + m) * 2 + p, devices, stride=step), :] for c in range(2)],
             axis=0,
         )
-        turned = both.T.astype(BF16)
+        turned = both.astype(BF16).T
         half = turned.shape[0] // 2
         halves.append(jnp.concatenate([turned[:half], turned[half:]], axis=1))
     return jnp.concatenate(halves, axis=0)
@@ -120,88 +127,120 @@
         store.wait()
 
 
+def coefs_kernel(counts_ref, mixing_ref, out_ref):
+    size = mixing_ref.shape[5]
+    wave = lax.broadcasted_iota(jnp.int32, (2, size), 1)
+    place = lax.broadcasted_iota(jnp.int32, (2, size), 0)
+    radial = jnp.minimum(wave, size - wave)
+    for f in range(mixing_ref.shape[0]):
+        passing = radial <= jnp.where(place == 0, counts_ref[f, 0], counts_ref[f, 1])
+        for o in range(mixing_ref.shape[2]):
+            for i in range(mixing_ref.shape[3]):
+                a = jnp.where(passing, mixing_ref[f, 0, o, i], 0.0)
+                b = jnp.where(passing, mixing_ref[f, 1, o, i], 0.0)
+                out_ref[f, 0, o, i] = a
+                out_ref[f, 1, o, i] = a + b
+                out_ref[f, 2, o, i] = b - a
+
+
 def middle_kernel(
-    devices,
-    counts_ref,
-    in_ref,
-    mixing_ref,
-    fwd_ref,
-    inv_ref,
-    out_ref,
-    down_ref,
-    rows_ref,
-    k_ref,
-    block_ref,
-    out_sems,
+    devices, in_ref, coefs_ref, fwd_ref, inv_ref, out_ref, down_ref, rows_ref, k_ref, mixed_ref,
+    block_ref, out_sems,
 ):
-    bins, _, comps = mixing_ref.shape[:3]
-    size = mixing_ref.shape[5]
+    bins, _, comps = coefs_ref.shape[:3]
+    size = coefs_ref.shape[5]
     shots = in_ref.shape[2] // 2
-    wave = lax.broadcasted_iota(jnp.int32, (1, size), 1)
-    radial = jnp.minimum(wave, size - wave)
-    stores = []
-    for f in range(bins):
-        take(rows_ref, in_ref, 2 * comps * 2, f)
-        for m in range(comps):
-            k_ref[f, m] = dot(gathered(rows_ref, devices, comps, f, m), fwd_ref[...], NN)
-        for o in range(comps):
-            parts = []
-            for p in range(2):
-                passing = (radial <= counts_ref[f, p]).astype(F32)
-                span = pl.ds(p * shots, shots)
-                real = imag = None
+
+    def transformed(f, m):
+        k = dot(gathered(rows_ref, devices, comps, f, m), fwd_ref[...], NN)
+        k_ref[f, m, :, 0 : 2 * size] = k
+        k_ref[f, m, :, 2 * size : 3 * size] = k[:, :size] + k[:, size:]
+
+    def mixed(f, o):
+        into = down_ref.at[f] if o == 1 else mixed_ref.at[f, o]
+        for p in range(2):
+            for start in range(p * shots, (p + 1) * shots, CHUNK):
+                span = slice(start, start + CHUNK)
+                both = real = imag = None
                 for i in range(comps):
-                    a = mixing_ref[f, 0, o, i, p : p + 1, :] * passing
-                    b = mixing_ref[f, 1, o, i, p : p + 1, :] * passing
-                    kr = k_ref[f, i, span, 0:size]
-                    ki = k_ref[f, i, span, size : 2 * size]
-                    r = a * kr - b * ki
-                    s = a * ki + b * kr
+                    a, u, v = (coefs_ref[f, c, o, i, p : p + 1, :] for c in range(3))
+                    q = a * k_ref[f, i, span, 2 * size : 3 * size]
+                    r = u * k_ref[f, i, span, size : 2 * size]
+                    s = v * k_ref[f, i, span, 0:size]
+                    both = q if both is None else both + q
                     real = r if real is None else real + r
                     imag = s if imag is None else imag + s
-                parts.append(jnp.concatenate([real, imag], axis=1).astype(BF16))
-            mixed = jnp.concatenate(parts, axis=0)
-            if o == 1:
-                down_ref[f] = mixed
-            spread(rows_ref, devices, comps, f, o, dot(inv_ref[...], mixed, NT))
+                into[span, 0:size] = (both - real).astype(BF16)
+                into[span, size : 2 * size] = (both + imag).astype(BF16)
+
+    def back(f, o):
+        into = down_ref.at[f] if o == 1 else mixed_ref.at[f, o]
+        spread(rows_ref, devices, comps, f, o, dot(inv_ref[...], into[...], NT))
+
+    stores = []
+    take(rows_ref, in_ref, 2 * comps * 2, 0)
+    for m in range(comps):
+        transformed(0, m)
+    for f in range(bins):
+        if f + 1 < bins:
+            take(rows_ref, in_ref, 2 * comps * 2, f + 1)
+        for o in range(comps):
+            if f + 1 < bins:
+                transformed(f + 1, o)
+            mixed(f, o)
+            if o > 0:
+                back(f, o - 1)
+        back(f, comps - 1)
         stores.append(put(out_ref, block_ref, rows_ref, out_sems, f))
     for store in stores:
         store.wait()
 
 
-def gram_kernel(weight, down_ref, inv_ref, own_ref, *rest):
-    sent, gram_ref = rest[:-1], rest[-1]
-    bins = down_ref.shape[0]
+def gram_kernel(weight, down_ref, inv_ref, *rest):
+    *sent, lines_ref = rest
+    bins, lanes = down_ref.shape[:2]
     size = down_ref.shape[2] // 2
-    sy = own_ref.shape[0]
+    sy = sent[0].shape[0]
     share = size // (sy * SX)
     here = lax.axis_index("shot")
     here_x, here_y = lax.rem(here, SX), lax.div(here, SX)
-    lane = lax.broadcasted_iota(jnp.int32, (1, down_ref.shape[1]), 1)
-    shots = down_ref.shape[1] // 2
-    for f in range(bins):
-        spaced = dot(inv_ref[...], down_ref[f], NT).astype(BF16)
-        real, imag = spaced[:size], spaced[size:]
-        zero = jnp.zeros_like(real)
-        left = jnp.concatenate([real, imag], axis=1)
-        right = jnp.concatenate([left, jnp.concatenate([-imag, real], axis=1)], axis=0)
+    lane = lax.broadcasted_iota(jnp.int32, (1, lanes), 1)
+    keep = [(lane >= p * lanes // 2) & (lane < (p + 1) * lanes // 2) for p in range(2)]
+    starts = []
+    for t in range(SX):
+        for h in range(sy):
+            x, y = lax.rem(here_x + t, SX), lax.rem(here_y + h, sy)
+            starts.append(pl.multiple_of((y * SX + x) * share, share))
+    for f in range(bins):
+        lines_ref[f] = dot(inv_ref[...], down_ref[f], NT).astype(BF16)
+    prods = []
+    for f in range(bins):
+        real, imag = lines_ref[f, :size], lines_ref[f, size:]
+        right = jnp.concatenate(
+            [jnp.concatenate([real, imag], axis=1), jnp.concatenate([-imag, real], axis=1)],
+            axis=0,
+        )
+        parts = [
+            jnp.concatenate(
+                [lines_ref[f, pl.ds(c * size + start, share), :] for start in starts], axis=0
+            )
+            for c in range(2)
+        ]
+        left = [
+            jnp.concatenate([jnp.where(k, q, jnp.zeros_like(q)) for q in parts], axis=1)
+            for k in keep
+        ]
+        prods.append(dot(jnp.concatenate(left, axis=0), right, NT))
+    for f in range(bins):
         for p in range(2):
-            keep = (lane >= p * shots) & (lane < (p + 1) * shots)
-            part = jnp.concatenate(
-                [jnp.where(keep, real, zero), jnp.where(keep, imag, zero)], axis=1
-            )
-            prod = dot(part, right, NT) * weight
-            for c in range(2):
-                gram_ref[(f * 2 + c) * 2 + p] = prod[:, c * size : (c + 1) * size]
-    for t, ref in enumerate((own_ref, *sent)):
-        for h in range(sy):
-            x = lax.rem(here_x + t, SX)
-            y = lax.rem(here_y + h, sy)
-            start = pl.multiple_of((y * SX + x) * share, share)
-            for g in range(gram_ref.shape[0]):
-                ref[h, g * share : (g + 1) * share, :] = gram_ref[
-                    g, pl.ds(start, share), :
-                ].astype(ref.dtype)
+            for n in range(len(starts)):
+                ref = sent[n // sy]
+                row = p * size + n * share
+                for c in range(2):
+                    g = (f * 2 + c) * 2 + p
+                    ref[n % sy, g * share : (g + 1) * share, :] = (
+                        prods[f][row : row + share, c * size : (c + 1) * size] * weight
+                    ).astype(ref.dtype)
 
 
 def backward_kernel(devices, in_ref, table_ref, out_ref, rows_ref, res_ref, sems):
@@ -216,13 +255,15 @@
                     res_ref[f, d, m, l] = res[
                         l * shots : (l + 1) * shots, d * size : (d + 1) * size
                     ]
-            store = pltpu.make_async_copy(
-                res_ref.at[f, :, m], out_ref.at[f, :, m], sems.at[f * comps + m]
-            )
-            store.start()
-            stores.append(store)
+        store = pltpu.make_async_copy(res_ref.at[f], out_ref.at[f], sems.at[f])
+        store.start()
+        stores.append(store)
     for store in stores:
         store.wait()
+
+
+def exchange(blocks):
+    return lax.all_to_all(blocks, "rx", 0, 0, tiled=True, axis_index_groups=[ORDER])
 
 
 def params():
@@ -262,22 +303,32 @@
         ],
         name="forward",
     )(data, out_rows(forward_y, 2))
-    pencils = lax.all_to_all(sent, "rx", 0, 0, tiled=True)
+    pencils = exchange(sent)
+    coefs = pl.pallas_call(
+        coefs_kernel,
+        out_shape=jax.ShapeDtypeStruct((bins, 3, comps, comps, 2, rx), F32),
+        in_specs=[pl.BlockSpec(memory_space=pltpu.SMEM), vmem],
+        out_specs=vmem,
+        compiler_params=params(),
+        cost_estimate=pl.CostEstimate(flops=10**6, bytes_accessed=10**6, transcendentals=0),
+        name="coefs",
+    )(counts, mixing)
     spaced, down = pl.pallas_call(
         functools.partial(middle_kernel, devices),
         out_shape=(blocks, jax.ShapeDtypeStruct((bins, lanes, 2 * rx), BF16)),
-        in_specs=[pl.BlockSpec(memory_space=pltpu.SMEM), vmem, vmem, vmem, vmem],
+        in_specs=[vmem, vmem, vmem, vmem],
         out_specs=(outside, vmem),
         scratch_shapes=[
             rows,
-            pltpu.VMEM((bins, comps, lanes, 2 * rx), F32),
+            pltpu.VMEM((bins, comps, lanes, 3 * rx), F32),
+            pltpu.VMEM((bins, comps, lanes, 2 * rx), BF16),
             block,
             pltpu.SemaphoreType.DMA((bins,)),
         ],
         compiler_params=params(),
         name="middle",
-    )(counts, pencils, mixing, in_rows(forward_x, 2), out_rows(inverse_x, 2))
-    returned = lax.all_to_all(spaced, "rx", 0, 0, tiled=True)
+    )(pencils, coefs, in_rows(forward_x, 2), out_rows(inverse_x, 2))
+    returned = exchange(spaced)
 
     sy = shot_devices // SX
     share = rx // shot_devices
@@ -288,7 +339,7 @@
         + [jax.ShapeDtypeStruct(part, BF16)] * (SX - 1),
         in_specs=[vmem, vmem],
         out_specs=[vmem] * SX,
-        scratch_shapes=[pltpu.VMEM((bins * 2 * 2, rx, rx), F32)],
+        scratch_shapes=[pltpu.VMEM((bins, 2 * rx, lanes), BF16)],
         compiler_params=params(),
         cost_estimate=pl.CostEstimate(flops=10**8, bytes_accessed=10**6, transcendentals=0),
         name="gram",
@@ -309,7 +360,7 @@
         out_shape=fields_shape,
         in_specs=[vmem, vmem],
         out_specs=outside,
-        scratch_shapes=[rows, pltpu.VMEM(data.shape, BF16), pltpu.SemaphoreType.DMA((bins * comps,))],
+        scratch_shapes=[rows, pltpu.VMEM(data.shape, BF16), pltpu.SemaphoreType.DMA((bins,))],
         compiler_params=params(),
         name="backward",
     )

time: 78.5 us -> 77.6 us (0.989)
  the two profiles are of different devices: /device:TPU:8 before, /device:TPU:6 now
where the time goes in v3:
time: 77.6 us; the launch traced here: 77.1 us
  starting transfers between devices  38.2 us (49%)
  waiting for transfers between devices  30 us (39%)
  Pallas kernels  7.28 us (9%)
  between operations  0.8 us (1%)
    all_to_all x2, starting transfers between devices, exchange(): lax.all_to_all(blocks, 'rx', 0, 0, tiled=True, axis_index_groups=[ORDER])  22.9 us
    all_to_all x2, waiting for transfers between devices, exchange(): lax.all_to_all(blocks, 'rx', 0, 0, tiled=True, axis_index_groups=[ORDER])  20.3 us
    ppermute x3, starting transfers between devices, per_device(): total = total + lax.ppermute(parts[t - 1], 'shot', pairs).astype(F32)  8.62 us
    ppermute x1, starting transfers between devices, per_device(): far = lax.ppermute(total[h].astype(BF16), 'shot', pairs)  6.63 us
    ppermute x3, waiting for transfers between devices, per_device(): total = total + lax.ppermute(parts[t - 1], 'shot', pairs).astype(F32)  5.78 us
    ppermute x1, waiting for transfers between devices, per_device(): far = lax.ppermute(total[h].astype(BF16), 'shot', pairs)  3.91 us
    pallas_call x1, Pallas kernels, per_device(): pl.pallas_call(functools.partial(forward_kernel, devices), out_shape=bloc...  2.7 us
    pallas_call x1, Pallas kernels, per_device(): pl.pallas_call(functools.partial(middle_kernel, devices), out_shape=(bloc...  2.15 us
  transfers between devices with their start and end apart: 6, of which 4 were waited for; matrix products, arithmetic and copies ran while one was open for 1% of the time, Pallas kernels for 2%

profile of v3, /device:TPU:6, one launch (start us, length us, event | category | flops | bytes accessed | tf_op | source)
XLA Modules:
  0.0 77.1 jit_solution(12175237088788200022)
XLA Ops:
  0.6 2.7 %forward.1 = bf16[64,48,128]{2,1,0:T(8,128)(2,1)} custom-call(bf16[3,2,4,2,64,128]{5,4,3,2,1,0:T(8,128)(2,1)} %data_ref.1, bf16[256,256]{1,0:T(8,128)(2,1)} %constant.10.clone.table_ref), custom_call_target="tpu_custom_call" | custom-call | tf_op jit(solution)/shard_map/forward/pallas_call | solution.py:291
  3.3 0.0 copy-start.5
  3.3 0.0 copy-start.3
  3.4 0.0 copy-start.1
  3.4 16.1 %all-to-all-start = ((bf16[64,48,128]{2,1,0:T(8,128)(2,1)}), bf16[64,48,128]{2,1,0:T(8,128)(2,1)S(1)}, u32[]{:S(2)}, u32[]{:S(2)}) async-start(bf16[64,48,128]{2,1,0:T(8,128)(2,1)} %forward.1), calls=%async_computation | async-start | bytes 1572864 | tf_op jit(solution)/shard_map/all_to_all | solution.py:266
  19.5 0.0 copy-done.5
  19.5 0.0 copy-start
  19.5 0.1 copy.10.counts_ref
  19.6 0.0 copy-done.3
  19.6 0.6 coefs.1.coefs_ref
  20.3 20.3 %all-to-all-done.in_ref = bf16[64,48,128]{2,1,0:T(8,128)(2,1)S(1)} async-done(((bf16[64,48,128]{2,1,0:T(8,128)(2,1)}), bf16[64,48,128]{2,1,0:T(8,128)(2,1)S(1)}, u32[]{:S(2)}, u32[]{:S(2)}) %all-to-all-start) | async-done | bytes 786464 | tf_op jit(solution)/shard_map/all_to_all | solution.py:266
  40.6 0.0 copy-done.1
  40.6 0.0 copy-done
  40.6 2.1 %middle.1 = (bf16[64,48,128]{2,1,0:T(8,128)(2,1)}, bf16[3,128,256]{2,1,0:T(8,128)(2,1)S(1)}) custom-call(bf16[64,48,128]{2,1,0:T(8,128)(2,1)S(1)} %all-to-all-done.in_ref, f32[3,3,4,4,2,128]{5,4,3,2,1,0:T(2,128)S(1)} %coefs.1.coefs_ref, bf16[256,256]{1,0:T(8,128)(2,1)S(1)} %copy-done.1, bf16[256,256]{1,0:T(8,128)(2,1)S(1)} %copy-done), custom_call_target="tpu_custom_call" | custom-call | tf_op jit(solution)/shard_map/middle/pallas_call | solution.py:316
  42.8 0.0 copy-start.4
  42.8 6.8 %all-to-all-start.1 = ((bf16[64,48,128]{2,1,0:T(8,128)(2,1)}), bf16[64,48,128]{2,1,0:T(8,128)(2,1)S(1)}, u32[]{:S(2)}, u32[]{:S(2)}) async-start(bf16[64,48,128]{2,1,0:T(8,128)(2,1)} %get-tuple-element.8), calls=%async_computation.1 | async-start | bytes 1572864 | tf_op jit(solution)/shard_map/all_to_all | solution.py:266
  49.6 0.0 copy-done.4
  49.6 0.6 gram.1
  50.2 2.4 %collective-permute-start = (bf16[2,192,128]{2,1,0:T(8,128)(2,1)S(1)}, bf16[2,192,128]{2,1,0:T(8,128)(2,1)S(1)}, u32[]{:S(2)}, u32[]{:S(2)}) collective-permute-start(bf16[2,192,128]{2,1,0:T(8,128)(2,1)S(1)} %get-tuple-element.11), channel_id=1, source_target_pairs={{0,1},{1,2},{2,3},{3,0},{4,5},{5,6},{6,7},{7,4},{8,9},{9,10},{10,1... | collective-permute-start | bytes 294920 | tf_op jit(solution)/shard_map/ppermute | solution.py:350
  52.6 4.3 %collective-permute-start.1 = (bf16[2,192,128]{2,1,0:T(8,128)(2,1)S(1)}, bf16[2,192,128]{2,1,0:T(8,128)(2,1)S(1)}, u32[]{:S(2)}, u32[]{:S(2)}) collective-permute-start(bf16[2,192,128]{2,1,0:T(8,128)(2,1)S(1)} %get-tuple-element.12), channel_id=1, source_target_pairs={{0,2},{1,3},{2,0},{3,1},{4,6},{5,7},{6,4},{7,5},{8,10},{9,11},{10,... | collective-permute-start | bytes 294920 | tf_op jit(solution)/shard_map/ppermute | solution.py:350
  56.9 1.9 %collective-permute-start.2 = (bf16[2,192,128]{2,1,0:T(8,128)(2,1)S(1)}, bf16[2,192,128]{2,1,0:T(8,128)(2,1)S(1)}, u32[]{:S(2)}, u32[]{:S(2)}) collective-permute-start(bf16[2,192,128]{2,1,0:T(8,128)(2,1)S(1)} %get-tuple-element.13), channel_id=1, source_target_pairs={{0,3},{1,0},{2,1},{3,2},{4,7},{5,4},{6,5},{7,6},{8,11},{9,8},{10,9... | collective-permute-start | bytes 294920 | tf_op jit(solution)/shard_map/ppermute | solution.py:350
  58.8 0.0 collective-permute-done
  58.8 1.8 %collective-permute-done.1 = bf16[2,192,128]{2,1,0:T(8,128)(2,1)S(1)} collective-permute-done((bf16[2,192,128]{2,1,0:T(8,128)(2,1)S(1)}, bf16[2,192,128]{2,1,0:T(8,128)(2,1)S(1)}, u32[]{:S(2)}, u32[]{:S(2)}) %collective-permute-start.1) | collective-permute-done | bytes 98336 | tf_op jit(solution)/shard_map/ppermute | solution.py:350
  60.7 3.9 %collective-permute-done.2 = bf16[2,192,128]{2,1,0:T(8,128)(2,1)S(1)} collective-permute-done((bf16[2,192,128]{2,1,0:T(8,128)(2,1)S(1)}, bf16[2,192,128]{2,1,0:T(8,128)(2,1)S(1)}, u32[]{:S(2)}, u32[]{:S(2)}) %collective-permute-start.2) | collective-permute-done | bytes 98336 | tf_op jit(solution)/shard_map/ppermute | solution.py:350
  64.7 0.0 copy-start.2
  64.7 6.6 %collective-permute-start.3 = (bf16[192,128]{1,0:T(8,128)(2,1)S(1)}, bf16[192,128]{1,0:T(8,128)(2,1)S(1)}, u32[]{:S(2)}, u32[]{:S(2)}) collective-permute-start(bf16[192,128]{1,0:T(8,128)(2,1)S(1)} %fusion.1), channel_id=1, source_target_pairs={{0,4},{1,5},{2,6},{3,7},{4,0},{5,1},{6,2},{7,3},{8,12},{9,13},{10,... | collective-permute-start | bytes 147464 | tf_op jit(solution)/shard_map/ppermute | solution.py:354
  71.3 3.9 %collective-permute-done.3 = bf16[192,128]{1,0:T(8,128)(2,1)S(1)} collective-permute-done((bf16[192,128]{1,0:T(8,128)(2,1)S(1)}, bf16[192,128]{1,0:T(8,128)(2,1)S(1)}, u32[]{:S(2)}, u32[]{:S(2)}) %collective-permute-start.3) | collective-permute-done | bytes 49184 | tf_op jit(solution)/shard_map/ppermute | solution.py:354
  75.3 0.7 fusion
  75.9 0.0 all-to-all-done.1.in_ref
  75.9 0.0 copy-done.2
  75.9 1.2 %backward.1 = bf16[3,2,4,2,64,128]{5,4,3,2,1,0:T(8,128)(2,1)} custom-call(bf16[64,48,128]{2,1,0:T(8,128)(2,1)S(1)} %all-to-all-done.1.in_ref, bf16[256,256]{1,0:T(8,128)(2,1)S(1)} %copy-done.2), custom_call_target="tpu_custom_call" | custom-call | tf_op jit(solution)/shard_map/backward/pallas_call | solution.py:367
  (2 shorter events, 0.1 us)
Async XLA Ops:
  3.3 16.2 %copy-start.5 = (s32[3,2]{0,1:T(2,128)S(1)}, s32[3,2]{0,1:T(2,128)}, u32[]{:S(2)}) copy-start(s32[3,2]{0,1:T(2,128)} %param.10) | copy-start | bytes 76
  3.3 16.3 %copy-start.3 = (f32[3,2,4,4,2,128]{5,4,3,2,1,0:T(2,128)S(1)}, f32[3,2,4,4,2,128]{5,4,3,2,1,0:T(2,128)}, u32[]{:S(2)}) copy-start(f32[3,2,4,4,2,128]{5,4,3,2,1,0:T(2,128)} %mixing_ref.1) | copy-start | bytes 294916
  3.4 37.2 %copy-start.1 = (bf16[256,256]{1,0:T(8,128)(2,1)S(1)}, bf16[256,256]{1,0:T(8,128)(2,1)}, u32[]{:S(2)}) copy-start(bf16[256,256]{1,0:T(8,128)(2,1)} %constant.11.clone.fwd_ref) | copy-start | bytes 393220
  3.4 37.2 %all-to-all-start = ((bf16[64,48,128]{2,1,0:T(8,128)(2,1)}), bf16[64,48,128]{2,1,0:T(8,128)(2,1)S(1)}, u32[]{:S(2)}, u32[]{:S(2)}) async-start(bf16[64,48,128]{2,1,0:T(8,128)(2,1)} %forward.1), calls=%async_computation | async-start | bytes 1572864 | tf_op jit(solution)/shard_map/all_to_all | solution.py:266
  19.5 21.1 %copy-start = (bf16[256,256]{1,0:T(8,128)(2,1)S(1)}, bf16[256,256]{1,0:T(8,128)(2,1)}, u32[]{:S(2)}) copy-start(bf16[256,256]{1,0:T(8,128)(2,1)} %constant.12.clone.inv_ref) | copy-start | bytes 393220
  42.8 6.8 %copy-start.4 = (bf16[256,256]{1,0:T(8,128)(2,1)S(1)}, bf16[256,256]{1,0:T(8,128)(2,1)}, u32[]{:S(2)}) copy-start(bf16[256,256]{1,0:T(8,128)(2,1)} %constant.13.clone.inv_ref) | copy-start | bytes 393220
  42.8 33.1 %all-to-all-start.1 = ((bf16[64,48,128]{2,1,0:T(8,128)(2,1)}), bf16[64,48,128]{2,1,0:T(8,128)(2,1)S(1)}, u32[]{:S(2)}, u32[]{:S(2)}) async-start(bf16[64,48,128]{2,1,0:T(8,128)(2,1)} %get-tuple-element.8), calls=%async_computation.1 | async-start | bytes 1572864 | tf_op jit(solution)/shard_map/all_to_all | solution.py:266
  50.2 8.7 %collective-permute-start = (bf16[2,192,128]{2,1,0:T(8,128)(2,1)S(1)}, bf16[2,192,128]{2,1,0:T(8,128)(2,1)S(1)}, u32[]{:S(2)}, u32[]{:S(2)}) collective-permute-start(bf16[2,192,128]{2,1,0:T(8,128)(2,1)S(1)} %get-tuple-element.11), channel_id=1, source_target_pairs={{0,1},{1,2},{2,3},{3,0},{4,5},{5,6},{6,7},{7,4},{8,9},{9,10},{10,1... | collective-permute-start | bytes 294920 | tf_op jit(solution)/shard_map/ppermute | solution.py:350
  52.6 8.1 %collective-permute-start.1 = (bf16[2,192,128]{2,1,0:T(8,128)(2,1)S(1)}, bf16[2,192,128]{2,1,0:T(8,128)(2,1)S(1)}, u32[]{:S(2)}, u32[]{:S(2)}) collective-permute-start(bf16[2,192,128]{2,1,0:T(8,128)(2,1)S(1)} %get-tuple-element.12), channel_id=1, source_target_pairs={{0,2},{1,3},{2,0},{3,1},{4,6},{5,7},{6,4},{7,5},{8,10},{9,11},{10,... | collective-permute-start | bytes 294920 | tf_op jit(solution)/shard_map/ppermute | solution.py:350
  56.9 7.7 %collective-permute-start.2 = (bf16[2,192,128]{2,1,0:T(8,128)(2,1)S(1)}, bf16[2,192,128]{2,1,0:T(8,128)(2,1)S(1)}, u32[]{:S(2)}, u32[]{:S(2)}) collective-permute-start(bf16[2,192,128]{2,1,0:T(8,128)(2,1)S(1)} %get-tuple-element.13), channel_id=1, source_target_pairs={{0,3},{1,0},{2,1},{3,2},{4,7},{5,4},{6,5},{7,6},{8,11},{9,8},{10,9... | collective-permute-start | bytes 294920 | tf_op jit(solution)/shard_map/ppermute | solution.py:350
  64.7 11.2 %copy-start.2 = (bf16[256,256]{1,0:T(8,128)(2,1)S(1)}, bf16[256,256]{1,0:T(8,128)(2,1)}, u32[]{:S(2)}) copy-start(bf16[256,256]{1,0:T(8,128)(2,1)} %constant.14.clone.table_ref) | copy-start | bytes 393220
  64.7 10.5 %collective-permute-start.3 = (bf16[192,128]{1,0:T(8,128)(2,1)S(1)}, bf16[192,128]{1,0:T(8,128)(2,1)S(1)}, u32[]{:S(2)}, u32[]{:S(2)}) collective-permute-start(bf16[192,128]{1,0:T(8,128)(2,1)S(1)} %fusion.1), channel_id=1, source_target_pairs={{0,4},{1,5},{2,6},{3,7},{4,0},{5,1},{6,2},{7,3},{8,12},{9,13},{10,... | collective-permute-start | bytes 147464 | tf_op jit(solution)/shard_map/ppermute | solution.py:354
